TPU v7x, 256 devices: a whole 4x4x8 slice. The times are simulated.
256 devices in a mesh: seq: 16 (over z, x_lo), wr: 4 (over y), wc: 4 (over x_hi, core).
Axes of the slice: x: 4 (x_hi: 2, x_lo: 2; x = x_hi * 2 + x_lo), y: 4, z: 8, core: 2. Of those that a mesh axis runs over, the one named last changes fastest.
Arguments:
- tokens: bfloat16 [8192, 2048], P('seq', ('wr', 'wc')), may hold values from -6 to 6
- ln_gain: float32 [2, 2048], replicated, may hold values from 0.5 to 1.5
- w_branch: bfloat16 [2, 2048, 4096], P(None, None, ('wr', 'wc')), may hold values from -0.125 to 0.125
- w_outgate: bfloat16 [2, 2048, 4096], P(None, None, ('wr', 'wc')), may hold values from -0.125 to 0.125
- w_gates: bfloat16 [2, 2048, 8], replicated, may hold values from -0.125 to 0.125
- forget_bias: float32 [2, 4], replicated, may hold values from 3.2 to 11
- conv_weight: float32 [2, 4, 4096], P(None, None, ('wr', 'wc')), may hold values from -3 to 3
- conv_bias: float32 [2, 4096], P(None, ('wr', 'wc')), may hold values from -3 to 3
- w_query: float32 [2, 4, 4, 4, 256], P(None, 'wr'), may hold values from -3 to 3
- w_key: float32 [2, 4, 4, 4, 256], P(None, 'wr'), may hold values from -3 to 3
- w_value: float32 [2, 4, 4, 4, 256], P(None, 'wr', None, 'wc'), may hold values from -4 to 4
- skip_gain: float32 [2, 4096], P(None, ('wr', 'wc')), may hold values from 0.5 to 1.5
- norm_gain: float32 [2, 4096], P(None, ('wr', 'wc')), may hold values from 0.5 to 1.5
- w_down: bfloat16 [2, 4096, 2048], P(None, ('wr', 'wc')), may hold values from -0.125 to 0.125
- lengths: int32 [3], replicated, may hold values from 1 to 4096, 8192 in all
- request_prompt: int32 [32], P('seq'), may hold values from 0 to 2
Outputs:
- mixed: bfloat16 [8192, 2048], P('seq', ('wr', 'wc'))
- request_state: bfloat16 [2, 32, 4, 1024, 1024], P(None, 'seq', 'wr', None, 'wc')
- request_conv: bfloat16 [2, 32, 3, 4096], P(None, 'seq', None, ('wr', 'wc'))
Inputs may be any that keep to these rules, and one draw needn't show every extreme that they name: `lengths`: the 3 prompts lie end to end in order and fill all 8192 positions; the longest has exactly 4096 positions.
All inputs are finite; a program needn't handle non-finite values.
Results may differ from a plain program's by a relative error of at most 0.035.
Values may be sent and summed in bfloat16 or wider, within the bound.
A program may use at most 128 MiB of HBM per device.

v0:
```python
import jax
import jax.numpy as jnp
from jax import lax
from jax.sharding import PartitionSpec as P

HEADS = 4
CONV = 4
LAYERS = 2
PROMPTS = 3


EPSILON = 1e-05
GATE_CAP = 15.0
ROW_DIMS = (((0,), (0,)), ((), ()))
FEATURE_DIMS = (((1,), (1,)), ((), ()))


def shifted(value, axis, steps):
    count = lax.axis_size(axis)
    first, last = (max(0, -steps), min(count, count - steps))
    return lax.ppermute(value, axis, [(source, source + steps) for source in range(first, last)])


def entering_2(shard, axis, join, neutral):
    place = lax.axis_index(axis)
    gathered = jax.tree.map(
        lambda a, kind: lax.all_gather(a.astype(kind), axis), shard, (jnp.bfloat16, jnp.bfloat16)
    )
    state = jax.tree.map(lambda a, e: jnp.zeros_like(a) + jnp.asarray(e, a.dtype), shard, neutral)

    def one(step, state):
        return join(
            state,
            jax.tree.map(
                lambda a, own: lax.dynamic_index_in_dim(a, step, 0, False).astype(own.dtype),
                gathered,
                shard,
            ),
        )

    return lax.fori_loop(0, place, one, state)


def broadcast(shard, axis, root):
    mine = lax.axis_index(axis) == root
    return lax.psum(jnp.where(mine, shard, jnp.zeros_like(shard)), axis)


def norm_rows(source, gain_row):
    widened = source.astype(jnp.float32)
    row_mean = jnp.mean(widened, axis=1, keepdims=True)
    row_var = jnp.mean(widened * widened, axis=1, keepdims=True) - row_mean * row_mean
    return ((widened - row_mean) * lax.rsqrt(row_var + EPSILON) * gain_row).astype(jnp.bfloat16)


def segment_of(positions, lengths):
    bound_one = lengths[0]
    bound_two = lengths[0] + lengths[1]
    return (positions >= bound_one).astype(jnp.int32) + (positions >= bound_two).astype(jnp.int32)


def conv_rows(extended, ext_segment, segment, weight, bias_row):
    row_count = segment.shape[0]
    widened = extended.astype(jnp.float32)
    summed = jnp.zeros((row_count, widened.shape[1]), jnp.float32) + bias_row
    for back_step in range(weight.shape[0]):
        low_row = weight.shape[0] - 1 - back_step
        keep_row = (ext_segment[low_row : low_row + row_count] == segment).astype(jnp.float32)
        summed = (
            summed + weight[back_step] * widened[low_row : low_row + row_count] * keep_row[:, None]
        )
    return jax.nn.silu(summed).astype(jnp.bfloat16)


def block_mix(source, weight):
    row_count = source.shape[0]
    grouped = source.astype(jnp.float32).reshape(row_count, 4, -1)
    mixed = jnp.einsum("tig,ijg->tjg", grouped, weight, precision=lax.Precision.HIGHEST)
    return mixed.reshape(row_count, -1)


def block_terms(queries, key_rows, values, log_forget, in_gate, segment, prev_seg):
    row_count = queries.shape[0]
    cum_log = jnp.cumsum(log_forget)
    row_order = jnp.arange(row_count)
    allowed = (row_order[:, None] >= row_order[None, :]) & (segment[:, None] == segment[None, :])
    exponent = jnp.where(allowed, cum_log[:, None] - cum_log[None, :] + in_gate[None, :], -jnp.inf)
    scores = lax.dot_general(
        queries, key_rows, FEATURE_DIMS, preferred_element_type=jnp.float32
    ) * jnp.exp(exponent)
    in_block = jnp.dot(scores.astype(jnp.bfloat16), values, preferred_element_type=jnp.float32)
    carried = jnp.where(segment == prev_seg, jnp.exp(cum_log), 0.0)
    last_seg = segment[row_count - 1]
    weights = jnp.where(
        segment == last_seg, jnp.exp(cum_log[row_count - 1] - cum_log + in_gate), 0.0
    )
    weighted = (key_rows.astype(jnp.float32) * weights[:, None]).astype(jnp.bfloat16)
    increment = lax.dot_general(weighted, values, ROW_DIMS, preferred_element_type=jnp.float32)
    block_decay = jnp.where(last_seg == prev_seg, jnp.exp(cum_log[row_count - 1]), 0.0)
    return (in_block, carried, increment, block_decay)


def end_state(
    state_in, key_rows, values, cum_log, in_gate, segment, seg_before, local_end, prompt, holder
):
    end_cum = cum_log[local_end]
    entering = jnp.where(holder & (seg_before == prompt), jnp.exp(end_cum), 0.0)
    row_order = jnp.arange(segment.shape[0])
    chosen = holder & (segment == prompt) & (row_order <= local_end)
    weights = jnp.where(chosen, jnp.exp(end_cum - cum_log + in_gate), 0.0)
    weighted = (key_rows.astype(jnp.float32) * weights[:, None]).astype(jnp.bfloat16)
    return entering * state_in + lax.dot_general(
        weighted, values, ROW_DIMS, preferred_element_type=jnp.float32
    )


def combine_states(earlier, later):
    return (earlier[0] * later[0], later[0] * earlier[1] + later[1])


def body(
    tokens,
    ln_gain,
    w_branch,
    w_outgate,
    w_gates,
    forget_bias,
    conv_weight,
    conv_bias,
    w_query,
    w_key,
    w_value,
    skip_gain,
    norm_gain,
    w_down,
    lengths,
    request_prompt,
):
    tok_rows = tokens.shape[0]
    seq_count = lax.axis_size("seq")
    seq_index = lax.axis_index("seq")
    head_idx = lax.axis_index("wr")
    row_offset = seq_index * tok_rows
    total_rows = tok_rows * seq_count
    row_ids = jnp.arange(tok_rows, dtype=jnp.int32)
    positions = row_offset + row_ids
    segment = segment_of(positions, lengths)
    seg_before = jnp.where(row_offset > 0, segment_of(row_offset - 1, lengths), -1)
    rim_positions = row_offset - (CONV - 1) + jnp.arange(CONV - 1, dtype=jnp.int32)
    rim_segment = jnp.where(rim_positions >= 0, segment_of(rim_positions, lengths), -1)
    ext_segment = jnp.concatenate([rim_segment, segment])
    prompt_starts = [jnp.zeros((), jnp.int32), lengths[0], lengths[0] + lengths[1]]
    prompt_ends = [
        lengths[0] - 1,
        lengths[0] + lengths[1] - 1,
        jnp.zeros((), jnp.int32) + (total_rows - 1),
    ]
    head_mask = (jnp.arange(HEADS, dtype=jnp.int32) == head_idx).astype(jnp.float32)
    current = tokens
    sent_states = []
    sent_edges = []
    for layer_idx in range(LAYERS):
        gathered = lax.all_gather(current, ("wr", "wc"), axis=1, tiled=True)
        normed = norm_rows(gathered, ln_gain[layer_idx])
        branch = jnp.dot(normed, w_branch[layer_idx], preferred_element_type=jnp.float32).astype(
            jnp.bfloat16
        )
        outgate = jnp.dot(normed, w_outgate[layer_idx], preferred_element_type=jnp.float32)
        gate_pre = jnp.dot(normed, w_gates[layer_idx], preferred_element_type=jnp.float32)
        input_pre = jnp.sum(gate_pre[:, :HEADS] * head_mask, axis=1)
        forget_pre = jnp.sum((gate_pre[:, HEADS:] + forget_bias[layer_idx]) * head_mask, axis=1)
        in_gate = GATE_CAP * jnp.tanh(input_pre / GATE_CAP)
        log_forget = jax.nn.log_sigmoid(forget_pre)
        edge_in = shifted(branch[tok_rows - (CONV - 1) :], "seq", 1)
        extended = jnp.concatenate([edge_in, branch], axis=0)
        conv_act = conv_rows(
            extended, ext_segment, segment, conv_weight[layer_idx], conv_bias[layer_idx]
        )
        head_branch, head_act = (
            lax.all_gather(branch, "wc", axis=1, tiled=True),
            lax.all_gather(conv_act, "wc", axis=1, tiled=True),
        )
        head_width = head_act.shape[1]
        queries = block_mix(head_act, w_query[layer_idx, 0]).astype(jnp.bfloat16)
        key_rows = (block_mix(head_act, w_key[layer_idx, 0]) * head_width ** (-0.5)).astype(
            jnp.bfloat16
        )
        values = block_mix(head_branch, w_value[layer_idx, 0]).astype(jnp.bfloat16)
        prefix = jnp.zeros((head_width, values.shape[1]), jnp.float32)
        reach_all = jnp.ones((), jnp.float32)
        in_block, carried, increment, block_decay = block_terms(
            queries, key_rows, values, log_forget, in_gate, segment, seg_before
        )
        saved_parts = (in_block, carried, reach_all, prefix)
        prefix = block_decay * prefix + increment
        reach_all = block_decay * reach_all
        entering = entering_2(
            (reach_all, prefix),
            "seq",
            combine_states,
            (jnp.ones((), jnp.float32), jnp.zeros_like(prefix)),
        )[1]
        in_block, carried, reach_here, prefix_here = saved_parts
        state_here = (reach_here * entering + prefix_here).astype(jnp.bfloat16)
        hidden_parts = in_block + carried[:, None] * jnp.dot(
            queries, state_here, preferred_element_type=jnp.float32
        )
        sums_one, sums_two = lax.psum(
            (jnp.sum(hidden_parts, axis=1), jnp.sum(hidden_parts * hidden_parts, axis=1)), "wc"
        )
        row_mean = sums_one / head_width
        row_var = sums_two / head_width - row_mean * row_mean
        normal_rows = (hidden_parts - row_mean[:, None]) * lax.rsqrt(row_var + EPSILON)[:, None]
        gated = (
            (
                normal_rows * norm_gain[layer_idx]
                + skip_gain[layer_idx] * conv_act.astype(jnp.float32)
            )
            * jax.nn.silu(outgate)
        ).astype(jnp.bfloat16)
        term_rows = jnp.dot(gated, w_down[layer_idx], preferred_element_type=jnp.float32)
        summed = lax.psum_scatter(
            term_rows.astype(jnp.bfloat16), ("wr", "wc"), scatter_dimension=1, tiled=True
        ).astype(jnp.float32)
        current = (current.astype(jnp.float32) + summed).astype(jnp.bfloat16)
        cum_log = jnp.cumsum(log_forget)
        for prompt in range(PROMPTS):
            end_pos = prompt_ends[prompt]
            holder = (end_pos >= row_offset) & (end_pos < row_offset + tok_rows)
            local_end = jnp.clip(end_pos - row_offset, 0, tok_rows - 1)
            state_end = end_state(
                entering,
                key_rows,
                values,
                cum_log,
                in_gate,
                segment,
                seg_before,
                local_end,
                prompt,
                holder,
            )
            window = lax.dynamic_slice_in_dim(extended, local_end + 1, CONV - 1, 0)
            edge_pos = end_pos - (CONV - 2) + jnp.arange(CONV - 1, dtype=jnp.int32)
            edge_rows = jnp.where(
                ((edge_pos >= prompt_starts[prompt]) & holder)[:, None],
                window,
                jnp.zeros_like(window),
            )
            got_state, got_edge = (
                broadcast(state_end.astype(jnp.bfloat16), "seq", end_pos // tok_rows),
                broadcast(edge_rows, "seq", end_pos // tok_rows),
            )
            sent_states.append(got_state)
            sent_edges.append(got_edge)
    state_stack = jnp.stack(sent_states)
    edge_stack = jnp.stack(sent_edges)
    state_stack = state_stack.reshape(LAYERS, PROMPTS, state_stack.shape[1], state_stack.shape[2])
    edge_stack = edge_stack.reshape(LAYERS, PROMPTS, edge_stack.shape[1], edge_stack.shape[2])
    chooser = (request_prompt[:, None] == jnp.arange(PROMPTS, dtype=jnp.int32)[None, :]).astype(
        jnp.bfloat16
    )
    request_state = jnp.einsum(
        "rp,lphd->lrhd", chooser, state_stack, preferred_element_type=jnp.float32
    ).astype(jnp.bfloat16)[:, :, None]
    request_conv = jnp.einsum(
        "rp,lpkc->lrkc", chooser, edge_stack, preferred_element_type=jnp.float32
    ).astype(jnp.bfloat16)
    return (current, request_state, request_conv)


def solution(mesh):
    return jax.shard_map(
        body,
        mesh=mesh,
        in_specs=(
            P("seq", ("wr", "wc")),
            P(),
            P(None, None, ("wr", "wc")),
            P(None, None, ("wr", "wc")),
            P(),
            P(),
            P(None, None, ("wr", "wc")),
            P(None, ("wr", "wc")),
            P(None, "wr", None, None, None),
            P(None, "wr", None, None, None),
            P(None, "wr", None, "wc", None),
            P(None, ("wr", "wc")),
            P(None, ("wr", "wc")),
            P(None, ("wr", "wc"), None),
            P(),
            P("seq"),
        ),
        out_specs=(
            P("seq", ("wr", "wc")),
            P(None, "seq", "wr", None, "wc"),
            P(None, "seq", None, ("wr", "wc")),
        ),
        check_vma=False,
    )
```

profile of v0, /device:TPU:8, one launch (start us, length us, event | category | flops | bytes accessed | tf_op | source)
XLA Modules:
  0.0 1091.4 jit_solution(4009449505985787538)
XLA Ops:
  17.0 47.3 %all-gather.11.cloned.1.call-done = bf16[512,2048]{1,0:T(8,128)(2,1)} async-done(((bf16[512,128]{1,0:T(8,128)(2,1)}), bf16[512,2048]{1,0:T(8,128)(2,1)}) %all-gather.11.cloned.1.call-update) | async-done | bytes 2097168 | tf_op jit(solution)/shard_map/all_gather | solution.py:163
  84.0 8.9 all-gather.15.cloned.1.call-done
  98.0 19.7 %all-gather.13.cloned.1.call-done = bf16[512,1024]{1,0:T(8,128)(2,1)} async-done(((bf16[512,256]{1,0:T(8,128)(2,1)}), bf16[512,1024]{1,0:T(8,128)(2,1)}) %all-gather.13.cloned.1.call-update) | async-done | bytes 1048592 | tf_op jit(solution)/shard_map/all_gather | solution.py:181
  123.1 4.2 fusion.99
  144.5 38.4 %all-reduce = bf16[16]{0:T(256)(128)(2,1)S(1)} all-reduce(bf16[16]{0:T(256)(128)(2,1)} %dynamic-update-slice), channel_id=1, replica_groups=mesh['seq'=16,'wr'=4,'wc'=4] {'seq'}, use_global_device_ids=true, to_apply=%add | all-reduce | flops 16 | bytes 64
  188.3 3.2 fusion.53
  191.5 130.1 %all-gather.23.cloned.1.call-done = bf16[16384,256]{1,0:T(8,128)(2,1)} async-done(((bf16[1024,256]{1,0:T(8,128)(2,1)}), bf16[16384,256]{1,0:T(8,128)(2,1)}) %all-gather.23.cloned.1.call-update) | async-done | bytes 8388624 | tf_op jit(solution)/shard_map/all_gather | solution.py:27
  325.1 9.7 all-reduce.3
  335.5 5.5 convolution_convert_fusion.1
  340.9 3.9 copy.136
  344.9 114.6 %reduce-scatter.7.cloned.1.call-done = bf16[128,512]{1,0:T(8,128)(2,1)} async-done(((bf16[2048,512]{1,0:T(8,128)(2,1)}), bf16[128,512]{1,0:T(8,128)(2,1)}) %reduce-scatter.7.cloned.1.call-update) | async-done | bytes 131088
  461.4 51.8 %all-gather.17.cloned.1.call-done = bf16[512,2048]{1,0:T(8,128)(2,1)} async-done(((bf16[512,128]{1,0:T(8,128)(2,1)}), bf16[512,2048]{1,0:T(8,128)(2,1)}) %all-gather.17.cloned.1.call-update) | async-done | bytes 2097168 | tf_op jit(solution)/shard_map/all_gather | solution.py:163
  533.4 8.5 all-gather.21.cloned.1.call-done
  546.0 20.8 %all-gather.19.cloned.1.call-done = bf16[512,1024]{1,0:T(8,128)(2,1)} async-done(((bf16[512,256]{1,0:T(8,128)(2,1)}), bf16[512,1024]{1,0:T(8,128)(2,1)}) %all-gather.19.cloned.1.call-update) | async-done | bytes 1048592 | tf_op jit(solution)/shard_map/all_gather | solution.py:181
  569.9 4.2 fusion.96
  591.8 68.1 %all-reduce.4 = (bf16[16]{0:T(256)(128)(2,1)S(1)}, bf16[1,3,256]{2,1,0:T(4,128)(2,1)S(1)}, bf16[1,3,256]{2,1,0:T(4,128)(2,1)S(1)}, bf16[1,3,256]{2,1,0:T(4,128)(...) all-reduce(bf16[16]{0:T(256)(128)(2,1)S(1)} %dynamic-update-slice.1, ...), channel_id=1, replica_groups=mesh['seq'=16,'wr'=4,'wc'=4] {'seq'}, use_global_device_ids=true, to_apply=%add.1 | all-reduce | flops 4624 | bytes 18496
  665.2 3.3 fusion.52
  668.5 102.8 %all-gather.25.cloned.1.call-done = bf16[16384,256]{1,0:T(8,128)(2,1)} async-done(((bf16[1024,256]{1,0:T(8,128)(2,1)}), bf16[16384,256]{1,0:T(8,128)(2,1)}) %all-gather.25.cloned.1.call-update) | async-done | bytes 8388624 | tf_op jit(solution)/shard_map/all_gather | solution.py:27
  774.3 9.1 all-reduce.2
  783.4 6.1 convolution_convert_fusion
  789.5 3.9 copy.138
  799.6 3.4 fusion.19
  825.2 81.6 %reduce-scatter.9.cloned.1.call-done = bf16[128,512]{1,0:T(8,128)(2,1)} async-done(((bf16[2048,512]{1,0:T(8,128)(2,1)}), bf16[128,512]{1,0:T(8,128)(2,1)}) %reduce-scatter.9.cloned.1.call-update) | async-done | bytes 131088
  908.5 168.8 %all-reduce.8.cloned.1.call-done = (bf16[1,1024,256]{2,1,0:T(8,128)(2,1)}, bf16[1,1024,256]{2,1,0:T(8,128)(2,1)}, bf16[1,1024,256]{2,1,0:T(8,128)(2,1)}, bf16[1,...) async-done(((bf16[1,1024,256]{2,1,0:T(8,128)(2,1)}, bf16[1,1024,256]{2,1,0:T(8,128)(2,1)}, bf16[1,1024,256]{2,1,0:T(8,128)(2,1)}, ...) | async-done | bytes 3145744 | tf_op jit(solution)/shard_map/psum | solution.py:46
  (254 shorter events, 149.1 us)
Async XLA Ops:
  7.2 57.1 %all-gather.11.cloned.1.call-start = ((), (), s32[]{:S(2)}) async-start(), calls=%async_computation.2 | async-start | bytes 2228224 | tf_op jit(solution)/shard_map/all_gather | solution.py:163
  7.9 85.0 %all-gather.15.cloned.1.call-start = ((), (), s32[]{:S(2)}) async-start(), calls=%async_computation.4 | async-start | bytes 1310720 | tf_op jit(solution)/shard_map/all_gather | solution.py:180
  11.3 59.9 %copy-start.39 = (f32[4]{0:T(128)}, f32[4]{0:T(128)S(1)}, u32[]{:S(2)}) copy-start(f32[4]{0:T(128)S(1)} %compare_convert_fusion) | copy-start | bytes 52
  69.8 47.8 %all-gather.13.cloned.1.call-start = ((), (), s32[]{:S(2)}) async-start(), calls=%async_computation.3 | async-start | bytes 1310720 | tf_op jit(solution)/shard_map/all_gather | solution.py:181
  71.2 7.3 copy-start.23
  71.3 10.8 copy-start.24
  71.8 4.1 collective-permute-start
  75.7 8.3 copy-start.30
  75.9 8.1 copy-start.27
  77.1 244.5 %all-gather.23.cloned.1.call-start = ((), (), s32[]{:S(2)}) async-start(), calls=%async_computation.8 | async-start | bytes 8912896 | tf_op jit(solution)/shard_map/all_gather | solution.py:27
  138.3 321.3 %reduce-scatter.7.cloned.1.call-start = ((), (), s32[]{:S(2)}) async-start(), calls=%async_computation.10 | async-start | bytes 2228224
  344.9 115.7 %copy-start.17 = (bf16[512,128]{1,0:T(8,128)(2,1)S(1)}, bf16[512,128]{1,0:T(8,128)(2,1)}, u32[]{:S(2)}) copy-start(bf16[512,128]{1,0:T(8,128)(2,1)} %param.20) | copy-start | bytes 393220
  344.9 168.3 %all-gather.17.cloned.1.call-start = ((), (), s32[]{:S(2)}) async-start(), calls=%async_computation.5 | async-start | bytes 2228224 | tf_op jit(solution)/shard_map/all_gather | solution.py:163
  461.3 80.5 %all-gather.21.cloned.1.call-start = ((), (), s32[]{:S(2)}) async-start(), calls=%async_computation.7 | async-start | bytes 1310720 | tf_op jit(solution)/shard_map/all_gather | solution.py:180
  517.3 10.1 copy-start
  518.7 7.6 copy-start.26
  518.7 48.0 %all-gather.19.cloned.1.call-start = ((), (), s32[]{:S(2)}) async-start(), calls=%async_computation.6 | async-start | bytes 1310720 | tf_op jit(solution)/shard_map/all_gather | solution.py:181
  519.5 3.8 collective-permute-start.1
  526.1 245.2 %all-gather.25.cloned.1.call-start = ((), (), s32[]{:S(2)}) async-start(), calls=%async_computation.9 | async-start | bytes 8912896 | tf_op jit(solution)/shard_map/all_gather | solution.py:27
  586.7 320.1 %reduce-scatter.9.cloned.1.call-start = ((), (), s32[]{:S(2)}) async-start(), calls=%async_computation.11 | async-start | bytes 2228224
  771.6 11.8 %copy-start.44 = (f32[1,256]{1,0:T(1,128)S(1)}, f32[1,256]{1,0:T(1,128)}, u32[]{:S(2)}) copy-start(f32[1,256]{1,0:T(1,128)} %get-tuple-element.222) | copy-start | bytes 3076
  771.6 11.8 %copy-start.45 = (f32[1,256]{1,0:T(1,128)S(1)}, f32[1,256]{1,0:T(1,128)}, u32[]{:S(2)}) copy-start(f32[1,256]{1,0:T(1,128)} %get-tuple-element.220) | copy-start | bytes 3076
  793.4 283.9 %all-reduce.8.cloned.1.call-start = ((), (), s32[]{:S(2)}) async-start(), calls=%async_computation.12 | async-start | bytes 6291456 | tf_op jit(solution)/shard_map/psum | solution.py:46
  823.8 84.1 %copy-start.16 = (bf16[512,128]{1,0:T(8,128)(2,1)S(1)}, bf16[512,128]{1,0:T(8,128)(2,1)}, u32[]{:S(2)}) copy-start(bf16[512,128]{1,0:T(8,128)(2,1)} %add_convert_fusion.1) | copy-start | bytes 393220
  (39 other events, 125.6 us)
Sparse Core Ops, SparseCore 0:
  10.6 53.6 all-gather.10
  69.9 22.9 all-gather.14
  94.7 22.8 all-gather.12
  138.4 183.1 all-gather.22
  345.0 114.5 reduce-scatter.6
  463.0 50.1 all-gather.16
  518.8 22.9 all-gather.20
  543.8 22.8 all-gather.18
  586.8 184.3 all-gather.24
  793.6 113.2 reduce-scatter.8
  909.9 167.3 all-reduce.7
where the time goes:
time: 1100 us; the launch traced here: 1090 us
  waiting for transfers between devices  757 us (69%)
  blocking collectives  125 us (11%)
  local copies, waits for them, and re-layouts  79.5 us (7%)
  matrix products  59.7 us (5%)
  other arithmetic  39.7 us (4%)
  between operations  24.4 us (2%)
    all_gather x2, waiting for transfers between devices, entering_2(): lax.all_gather(a.astype(kind), axis)  233 us
    unnamed x13, waiting for transfers between devices  197 us
    psum x1, waiting for transfers between devices, broadcast(): return lax.psum(jnp.where(mine, shard, jnp.zeros_like(shard)), axis)  169 us
    unnamed x2, blocking collectives  106 us
    all_gather x2, waiting for transfers between devices, body(): gathered = lax.all_gather(current, ('wr', 'wc'), axis=1, tiled=True)  99.1 us
    all_gather x2, waiting for transfers between devices, body(): lax.all_gather(conv_act, 'wc', axis=1, tiled=True)  40.5 us
    unnamed x126, local copies, waits for them, and re-layouts  27.7 us
  transfers between devices with their start and end apart: 13, of which 12 were waited for; matrix products, arithmetic and copies ran while one was open for 8% of the time, Pallas kernels for 0%

commit v1 on v0

v1 whole, which is shorter than its diff:
```python
import jax
import jax.numpy as jnp
from jax import lax
from jax.experimental import pallas as pl
from jax.experimental.pallas import tpu as pltpu
from jax.sharding import PartitionSpec as P

HEADS = 4
CONV = 4
LAYERS = 2
PROMPTS = 3
SEQ = 16
SPLIT = 7

EPSILON = 1e-05
GATE_CAP = 15.0
FEATURE_DIMS = (((1,), (1,)), ((), ()))
ROW_DIMS = (((0,), (0,)), ((), ()))
MESH = pl.DeviceIdType.MESH
VM = pl.BlockSpec(memory_space=pltpu.VMEM)
DMA = pltpu.SemaphoreType.DMA


def params(collective):
    return pltpu.CompilerParams(
        collective_id=collective, has_side_effects=True, vmem_limit_bytes=48 * 1024 * 1024
    )


def greet(peers):
    barrier = pltpu.get_barrier_semaphore()
    for peer in peers:
        pl.semaphore_signal(barrier, inc=1, device_id=peer, device_id_type=MESH)
    pl.semaphore_wait(barrier, len(peers))


def copy_to(source, target, send, recv, peer):
    made = pltpu.make_async_remote_copy(
        src_ref=source, dst_ref=target, send_sem=send, recv_sem=recv, device_id=peer, device_id_type=MESH
    )
    made.start()
    return made


def plane():
    row, col = lax.axis_index("wr"), lax.axis_index("wc")
    core = lax.rem(col, 2)
    cross = lax.rem(col + 2, 4)
    mate = col + 1 - 2 * core
    return row, col, core, cross, mate


def plane_peers(row, cross, mate):
    return [{"wr": lax.rem(row + d, 4)} for d in (1, 2, 3)] + [{"wc": cross}, {"wc": mate}]


def gather_plane(own_ref, out_ref, send, recv):
    row, col, core, cross, mate = plane()
    mate_cross = lax.rem(mate + 2, 4)
    width = own_ref.shape[1]

    def block(r, c):
        return out_ref.at[:, pl.ds(pl.multiple_of((r * 4 + c) * width, width), width)]

    def move(source, r, c, slot, peer):
        return copy_to(source, block(r, c), send.at[slot], recv.at[slot], peer)

    rows = [lax.rem(row + d, 4) for d in range(4)]
    back = [lax.rem(row + 4 - d, 4) for d in range(4)]
    sent = {}
    sent[0] = move(own_ref, row, col, 0, {"wc": cross})
    for d in (1, 3, 2):
        sent[d] = move(own_ref, row, col, d, {"wr": rows[d]})
    sent[7] = move(own_ref, row, col, 7, {"wc": mate})
    sent[0].wait_recv()
    for d in (1, 3, 2):
        sent[3 + d] = move(block(row, cross), row, cross, 3 + d, {"wr": rows[d]})
    sent[8] = move(block(row, cross), row, cross, 8, {"wc": mate})
    for d in (1, 3, 2):
        sent[d].wait_recv()
        sent[8 + d] = move(block(back[d], col), back[d], col, 8 + d, {"wc": mate})
    for d in (1, 3, 2):
        sent[3 + d].wait_recv()
        sent[11 + d] = move(block(back[d], cross), back[d], cross, 11 + d, {"wc": mate})
    for slot in range(7, 15):
        sent[slot].wait_recv()
    for slot in range(15):
        sent[slot].wait_send()


def gather16(own):
    rows, width = own.shape

    def kernel(own_ref, out_ref, send, recv):
        row, col, core, cross, mate = plane()
        greet(plane_peers(row, cross, mate))
        out_ref[:, pl.ds(pl.multiple_of((row * 4 + col) * width, width), width)] = own_ref[...]
        gather_plane(own_ref, out_ref, send, recv)

    return pl.pallas_call(
        kernel,
        out_shape=jax.ShapeDtypeStruct((rows, width * 16), own.dtype),
        in_specs=[VM],
        out_specs=VM,
        scratch_shapes=[DMA((15,)), DMA((15,))],
        compiler_params=params(1),
        name="gather_tokens",
    )(own)


def gather_head(branch):
    rows, width = branch.shape
    rim = 16

    def kernel(own_ref, out_ref, rim_ref, send, recv):
        row, col, core, cross, mate = plane()
        place = lax.axis_index("seq")
        after = lax.rem(place + 1, SEQ)
        onward = [{"seq": after, "wc": lax.rem(col + j, 4)} for j in range(4)]
        before = lax.rem(place + SEQ - 1, SEQ)
        greet([{"wc": cross}, {"wc": mate}] + [{"seq": before, "wc": lax.rem(col + j, 4)} for j in range(4)])

        def block(ref, c):
            return ref.at[:, pl.ds(pl.multiple_of(c * width, width), width)]

        over = copy_to(own_ref, block(out_ref, col), send.at[0], recv.at[0], {"wc": cross})
        side = copy_to(own_ref, block(out_ref, col), send.at[1], recv.at[1], {"wc": mate})
        tails = [
            copy_to(own_ref.at[pl.ds(rows - rim, rim)], block(rim_ref, col), send.at[3 + j], recv.at[3 + j], onward[j])
            for j in range(4)
        ]
        out_ref[:, pl.ds(pl.multiple_of(col * width, width), width)] = own_ref[...]
        over.wait_recv()
        last = copy_to(block(out_ref, cross), block(out_ref, cross), send.at[2], recv.at[2], {"wc": mate})
        side.wait_recv()
        for tail in tails:
            tail.wait_recv()
        last.wait_recv()
        for made in [over, side, last] + tails:
            made.wait_send()

    return pl.pallas_call(
        kernel,
        out_shape=(
            jax.ShapeDtypeStruct((rows, width * 4), branch.dtype),
            jax.ShapeDtypeStruct((rim, width * 4), branch.dtype),
        ),
        in_specs=[VM],
        out_specs=(VM, VM),
        scratch_shapes=[DMA((7,)), DMA((7,))],
        compiler_params=params(2),
        name="gather_head",
    )(branch)


SMALL = 24


def scan_states(grown, ends_a, ends_b, small):
    spans, part, width = grown.shape

    def kernel(
        grown_ref, a_ref, b_ref, small_ref, state_ref, chosen_ref, edge_ref,
        got, got_a, got_b, got_small, going, total, send, recv, local,
    ):
        place = lax.axis_index("seq")
        peers = [lax.rem(place + d, SEQ) for d in range(SEQ)]
        greet([{"seq": peers[d]} for d in range(1, SEQ)])
        sent = [[], [], [], []]
        for d in range(1, SEQ):
            to = {"seq": peers[d]}
            sent[0].append(copy_to(small_ref, got_small.at[place], send.at[0, d], recv.at[0, d], to))
            sent[1].append(copy_to(grown_ref.at[peers[d]], got.at[place], send.at[1, d], recv.at[1, d], to))
        own = [
            pltpu.make_async_copy(small_ref, got_small.at[place], local.at[0]),
            pltpu.make_async_copy(grown_ref.at[place], got.at[place], local.at[1]),
            pltpu.make_async_copy(a_ref.at[place], got_a.at[place], local.at[2]),
        ]
        for made in own:
            made.start()
        for d in range(1, SEQ):
            to = {"seq": peers[d]}
            sent[2].append(copy_to(a_ref.at[peers[d]], got_a.at[place], send.at[2, d], recv.at[2, d], to))
        b_copies = [
            pltpu.make_async_remote_copy(
                src_ref=b_ref.at[peers[d]], dst_ref=got_b, send_sem=send.at[4, d], recv_sem=recv.at[4, 0],
                device_id={"seq": peers[d]}, device_id_type=MESH,
            )
            for d in range(1, SEQ)
        ]

        @pl.when(place == SPLIT)
        def _():
            for made in b_copies:
                made.start()
            made = pltpu.make_async_copy(b_ref.at[place], got_b, local.at[3])
            made.start()
            made.wait()

        for made in own:
            made.wait()
        for made in sent[0] + sent[1]:
            made.wait_recv()
        state = jnp.zeros((part, width), jnp.float32)
        first = jnp.zeros((part, width), jnp.float32)
        second = jnp.zeros((part, width), jnp.float32)
        for k in range(SEQ):
            going[k] = state.astype(jnp.bfloat16)
            if k <= SPLIT:
                first = first + got_small[k, 10:11] * state
            if k >= SPLIT:
                second = second + got_small[k, 11:12] * state
            state = got_small[k, 9:10] * state + got[k].astype(jnp.float32)
        total[0] = first
        total[1] = second
        total[2] = state
        for d in range(1, SEQ):
            sent[3].append(
                copy_to(going.at[peers[d]], state_ref.at[place], send.at[3, d], recv.at[3, d], {"seq": peers[d]})
            )
        state_ref[place] = going[place]
        edge = got_small[0, 0:16]
        for k in range(1, SEQ):
            edge = edge + got_small[k, 0:16]
        edge_ref[...] = edge
        for made in sent[2]:
            made.wait_recv()

        @pl.when(place != SPLIT)
        def _():
            b_copies[0].wait_recv()

        first, second, third = total[0], total[1] + got_b[...].astype(jnp.float32), total[2]
        for k in range(SEQ):
            if k <= SPLIT:
                first = first + got_a[k].astype(jnp.float32)
            else:
                second = second + got_a[k].astype(jnp.float32)
        for k in range(SEQ):
            for j in range(2):
                row = 12 + 3 * j
                chosen_ref[k, j] = (
                    got_small[k, row : row + 1] * first
                    + got_small[k, row + 1 : row + 2] * second
                    + got_small[k, row + 2 : row + 3] * third
                ).astype(jnp.bfloat16)
        for made in sent[3]:
            made.wait_recv()
        for group in sent:
            for made in group:
                made.wait_send()

        @pl.when(place == SPLIT)
        def _():
            for made in b_copies:
                made.wait_send()

    return pl.pallas_call(
        kernel,
        out_shape=(
            jax.ShapeDtypeStruct((spans, part, width), jnp.bfloat16),
            jax.ShapeDtypeStruct((spans, 2, part, width), jnp.bfloat16),
            jax.ShapeDtypeStruct((16, width), jnp.float32),
        ),
        in_specs=[VM] * 4,
        out_specs=(VM, VM, VM),
        scratch_shapes=[
            pltpu.VMEM((spans, part, width), jnp.bfloat16),
            pltpu.VMEM((spans, part, width), jnp.bfloat16),
            pltpu.VMEM((part, width), jnp.bfloat16),
            pltpu.VMEM((spans, SMALL, width), jnp.float32),
            pltpu.VMEM((spans, part, width), jnp.bfloat16),
            pltpu.VMEM((3, part, width), jnp.float32),
            DMA((5, SEQ)),
            DMA((5, SEQ)),
            DMA((4,)),
        ],
        compiler_params=params(3),
        name="scan_states",
    )(grown, ends_a, ends_b, small)


def sum_wc(sums):
    def kernel(own_ref, out_ref, got, send, recv):
        col = lax.axis_index("wc")
        peers = [{"wc": lax.rem(col + d, 4)} for d in (1, 2, 3)]
        greet(peers)
        sent = [copy_to(own_ref, got.at[d], send.at[d], recv.at[d], peers[d]) for d in range(3)]
        for made in sent:
            made.wait()
        out_ref[...] = own_ref[...] + got[0] + got[1] + got[2]

    return pl.pallas_call(
        kernel,
        out_shape=jax.ShapeDtypeStruct(sums.shape, sums.dtype),
        in_specs=[VM],
        out_specs=VM,
        scratch_shapes=[pltpu.VMEM((3,) + sums.shape, sums.dtype), DMA((3,)), DMA((3,))],
        compiler_params=params(4),
        name="sum_wc",
    )(sums)


def reduce_plane(terms, current, chosen, gather):
    rows, width = current.shape
    spans, reqs, part, cols = chosen.shape

    def kernel(*refs):
        if gather:
            (term_ref, cur_ref, chosen_ref, new_ref, req_ref, out_ref, near, held, far, last, pair,
             send, recv, fsend, frecv, local, gsend, grecv) = refs
        else:
            (term_ref, cur_ref, chosen_ref, new_ref, req_ref, near, held, far, last, pair,
             send, recv, fsend, frecv, local) = refs
        place = lax.axis_index("seq")
        row, col, core, cross, mate = plane()
        spans_to = [lax.rem(place + d, SEQ) for d in range(SEQ)]
        greet(plane_peers(row, cross, mate) + [{"seq": spans_to[d]} for d in range(1, SEQ)])
        order = [2, 1, 3, 0]
        rows_to = [lax.rem(row + d, 4) for d in range(4)]

        def block(r, c):
            return pl.ds(pl.multiple_of((r * 4 + c) * width, width), width)

        first = []
        for i, d in enumerate(order):
            for h in range(2):
                first.append(
                    copy_to(
                        term_ref.at[:, block(rows_to[d], 2 * h + 1 - core)], near.at[2 * d + h],
                        send.at[2 * d + h], recv.at[2 * d + h], {"wc": mate},
                    )
                )
        side = [
            copy_to(chosen_ref.at[spans_to[d]], req_ref.at[:, place], fsend.at[d], frecv.at[d], {"seq": spans_to[d]})
            for d in range(1, SEQ)
        ]
        keep = pltpu.make_async_copy(chosen_ref.at[place], req_ref.at[:, place], local)
        keep.start()
        second = []
        for i, d in enumerate(order):
            for h in range(2):
                first[2 * i + h].wait_recv()
                total = term_ref[:, block(rows_to[d], 2 * h + core)].astype(jnp.float32) + near[2 * d + h].astype(
                    jnp.float32
                )
                if d > 0:
                    held[2 * d + h] = total.astype(jnp.bfloat16)
                else:
                    pair[h] = total
            if d > 0:
                second.append(
                    copy_to(
                        held.at[pl.ds(2 * d, 2)], far.at[d - 1], send.at[8 + d], recv.at[8 + d], {"wr": rows_to[d]}
                    )
                )
        for made in second:
            made.wait_recv()
        other = lax.rem(lax.div(col, 2) + 1, 2)
        for h in range(2):
            pair[h] = (
                pair[h]
                + far[0, h].astype(jnp.float32)
                + far[1, h].astype(jnp.float32)
                + far[2, h].astype(jnp.float32)
            )
        held[0] = pair[other].astype(jnp.bfloat16)
        third = copy_to(held.at[0], last, send.at[8], recv.at[8], {"wc": cross})
        third.wait_recv()
        new_ref[...] = (
            cur_ref[...].astype(jnp.float32) + (pair[1 - other] + last[...].astype(jnp.float32))
        ).astype(jnp.bfloat16)
        if gather:
            out_ref[:, block(row, col)] = new_ref[...]
            gather_plane(new_ref, out_ref, gsend, grecv)
        for made in side:
            made.wait_recv()
        keep.wait()
        for made in first + second + [third] + side:
            made.wait_send()

    shapes = [
        jax.ShapeDtypeStruct((rows, width), jnp.bfloat16),
        jax.ShapeDtypeStruct((reqs, spans, part, cols), jnp.bfloat16),
    ]
    scratch = [
        pltpu.VMEM((8, rows, width), jnp.bfloat16),
        pltpu.VMEM((8, rows, width), jnp.bfloat16),
        pltpu.VMEM((3, 2, rows, width), jnp.bfloat16),
        pltpu.VMEM((rows, width), jnp.bfloat16),
        pltpu.VMEM((2, rows, width), jnp.float32),
        DMA((12,)), DMA((12,)), DMA((SEQ,)), DMA((SEQ,)), DMA,
    ]
    if gather:
        shapes.append(jax.ShapeDtypeStruct((rows, width * 16), jnp.bfloat16))
        scratch += [DMA((15,)), DMA((15,))]
    return pl.pallas_call(
        kernel,
        out_shape=tuple(shapes),
        in_specs=[VM] * 3,
        out_specs=(VM,) * len(shapes),
        scratch_shapes=scratch,
        compiler_params=params(5 if gather else 6),
        name="reduce_gather" if gather else "reduce_last",
    )(terms, current, chosen)


def norm_rows(source, gain_row):
    widened = source.astype(jnp.float32)
    row_mean = jnp.mean(widened, axis=1, keepdims=True)
    row_var = jnp.mean(widened * widened, axis=1, keepdims=True) - row_mean * row_mean
    return ((widened - row_mean) * lax.rsqrt(row_var + EPSILON) * gain_row).astype(jnp.bfloat16)


def segment_of(positions, lengths):
    bound_one = lengths[0]
    bound_two = lengths[0] + lengths[1]
    return (positions >= bound_one).astype(jnp.int32) + (positions >= bound_two).astype(jnp.int32)


def conv_rows(extended, ext_segment, segment, weight, bias_row):
    row_count = segment.shape[0]
    widened = extended.astype(jnp.float32)
    summed = jnp.zeros((row_count, widened.shape[1]), jnp.float32) + bias_row
    for back_step in range(weight.shape[0]):
        low_row = weight.shape[0] - 1 - back_step
        keep_row = (ext_segment[low_row : low_row + row_count] == segment).astype(jnp.float32)
        summed = (
            summed + weight[back_step] * widened[low_row : low_row + row_count] * keep_row[:, None]
        )
    return jax.nn.silu(summed).astype(jnp.bfloat16)


def block_mix(source, weight):
    group = weight.shape[2]
    widened = source.astype(jnp.float32)
    blocks = [
        sum(widened[:, i * group : (i + 1) * group] * weight[i, j] for i in range(4))
        for j in range(weight.shape[1])
    ]
    return jnp.concatenate(blocks, axis=1) if len(blocks) > 1 else blocks[0]


def body(
    tokens, ln_gain, w_branch, w_outgate, w_gates, forget_bias, conv_weight, conv_bias, w_query, w_key, w_value,
    skip_gain, norm_gain, w_down, lengths, request_prompt,
):
    tok_rows = tokens.shape[0]
    seq_index = lax.axis_index("seq")
    head_idx = lax.axis_index("wr")
    col_idx = lax.axis_index("wc")
    row_offset = seq_index * tok_rows
    total_rows = tok_rows * SEQ
    positions = row_offset + jnp.arange(tok_rows, dtype=jnp.int32)
    segment = segment_of(positions, lengths)
    seg_before = jnp.where(row_offset > 0, segment_of(row_offset - 1, lengths), -1)
    rim_positions = row_offset - (CONV - 1) + jnp.arange(CONV - 1, dtype=jnp.int32)
    rim_segment = jnp.where(rim_positions >= 0, segment_of(rim_positions, lengths), -1)
    ext_segment = jnp.concatenate([rim_segment, segment])
    starts = [jnp.zeros((), jnp.int32), lengths[0], lengths[0] + lengths[1]]
    ends = [lengths[0] - 1, lengths[0] + lengths[1] - 1, jnp.zeros((), jnp.int32) + (total_rows - 1)]
    holders = [(end >= row_offset) & (end < row_offset + tok_rows) for end in ends]
    local_ends = [jnp.clip(end - row_offset, 0, tok_rows - 1) for end in ends]
    head_mask = (jnp.arange(HEADS, dtype=jnp.int32) == head_idx).astype(jnp.float32)
    row_order = jnp.arange(tok_rows)
    allowed = (row_order[:, None] >= row_order[None, :]) & (segment[:, None] == segment[None, :])
    choice = (request_prompt[:, None] == jnp.arange(PROMPTS, dtype=jnp.int32)[None, :]).astype(jnp.float32)
    conv_all = jnp.concatenate([conv_weight, conv_bias[:, None]], axis=1)
    conv_all = lax.all_gather(conv_all, "wc", axis=2, tiled=True)
    current = tokens
    gathered = gather16(tokens)
    states = []
    edges_out = []
    for layer in range(LAYERS):
        normed = norm_rows(gathered, ln_gain[layer])
        branch = jnp.dot(normed, w_branch[layer], preferred_element_type=jnp.float32).astype(jnp.bfloat16)
        outgate = jnp.dot(normed, w_outgate[layer], preferred_element_type=jnp.float32)
        gate_pre = jnp.dot(normed, w_gates[layer], preferred_element_type=jnp.float32)
        input_pre = jnp.sum(gate_pre[:, :HEADS] * head_mask, axis=1)
        forget_pre = jnp.sum((gate_pre[:, HEADS:] + forget_bias[layer]) * head_mask, axis=1)
        in_gate = GATE_CAP * jnp.tanh(input_pre / GATE_CAP)
        log_forget = jax.nn.log_sigmoid(forget_pre)
        head_branch, rim = gather_head(branch)
        width = branch.shape[1]
        extended = jnp.concatenate([rim[rim.shape[0] - (CONV - 1) :], head_branch], axis=0)
        head_act = conv_rows(extended, ext_segment, segment, conv_all[layer, :CONV], conv_all[layer, CONV])
        head_width = head_act.shape[1]
        queries = block_mix(head_act, w_query[layer, 0]).astype(jnp.bfloat16)
        key_rows = (block_mix(head_act, w_key[layer, 0]) * head_width ** (-0.5)).astype(jnp.bfloat16)
        values = block_mix(head_branch, w_value[layer, 0]).astype(jnp.bfloat16)
        cum_log = jnp.cumsum(log_forget)
        end_cum = cum_log[tok_rows - 1]
        last_seg = segment[tok_rows - 1]
        grow = jnp.where(segment == last_seg, jnp.exp(end_cum - cum_log + in_gate), 0.0)
        decay = jnp.where(last_seg == seg_before, jnp.exp(end_cum), 0.0)
        end_weights = []
        end_decays = []
        for prompt in range(2):
            local_cum = cum_log[local_ends[prompt]]
            chosen = holders[prompt] & (segment == prompt) & (row_order <= local_ends[prompt])
            end_weights.append(jnp.exp(jnp.where(chosen, local_cum - cum_log + in_gate, -jnp.inf)))
            end_decays.append(jnp.where(holders[prompt] & (seg_before == prompt), jnp.exp(local_cum), 0.0))
        weight_a = jnp.where(seq_index <= SPLIT, end_weights[0], end_weights[1])
        weights = jnp.stack([grow, weight_a, end_weights[1]], axis=1)
        weighted = (values.astype(jnp.float32)[:, None, :] * weights[:, :, None]).astype(jnp.bfloat16)
        sums = lax.dot_general(
            key_rows, weighted.reshape(tok_rows, -1), ROW_DIMS, preferred_element_type=jnp.float32
        ).astype(jnp.bfloat16)
        sums = sums.reshape(SEQ, head_width // SEQ, 3, width)
        own_extended = lax.dynamic_slice_in_dim(extended, col_idx * width, width, 1)
        small_rows = []
        for prompt in range(PROMPTS):
            window = lax.dynamic_slice_in_dim(own_extended, local_ends[prompt] + 1, CONV - 1, 0)
            edge_pos = ends[prompt] - (CONV - 2) + jnp.arange(CONV - 1, dtype=jnp.int32)
            keep = (edge_pos >= starts[prompt]) & holders[prompt]
            small_rows.append(jnp.where(keep[:, None], window.astype(jnp.float32), 0.0))
        scalars = jnp.concatenate([jnp.stack([decay] + end_decays), choice.reshape(-1), jnp.zeros((SMALL - 18,))])
        small = jnp.concatenate(small_rows + [jnp.broadcast_to(scalars[:, None], (scalars.shape[0], width))], axis=0)
        scores = lax.dot_general(queries, key_rows, FEATURE_DIMS, preferred_element_type=jnp.float32) * jnp.exp(
            jnp.where(allowed, cum_log[:, None] - cum_log[None, :] + in_gate[None, :], -jnp.inf)
        )
        in_block = jnp.dot(scores.astype(jnp.bfloat16), values, preferred_element_type=jnp.float32)
        carried = jnp.where(segment == seg_before, jnp.exp(cum_log), 0.0)
        state, chosen_states, edge_sum = scan_states(sums[:, :, 0], sums[:, :, 1], sums[:, :, 2], small)
        state_here = state.reshape(head_width, width)
        hidden = in_block + carried[:, None] * jnp.dot(queries, state_here, preferred_element_type=jnp.float32)
        stats = jnp.stack([jnp.sum(hidden, axis=1), jnp.sum(hidden * hidden, axis=1)])
        stats = sum_wc(jnp.concatenate([stats, jnp.zeros((6, tok_rows), jnp.float32)]))
        row_mean = stats[0] / head_width
        row_var = stats[1] / head_width - row_mean * row_mean
        normal_rows = (hidden - row_mean[:, None]) * lax.rsqrt(row_var + EPSILON)[:, None]
        conv_act = lax.dynamic_slice_in_dim(head_act, col_idx * width, width, 1)
        gated = (
            (normal_rows * norm_gain[layer] + skip_gain[layer] * conv_act.astype(jnp.float32))
            * jax.nn.silu(outgate)
        ).astype(jnp.bfloat16)
        terms = jnp.dot(gated, w_down[layer], preferred_element_type=jnp.float32).astype(jnp.bfloat16)
        made = reduce_plane(terms, current, chosen_states, layer + 1 < LAYERS)
        current = made[0]
        states.append(made[1].reshape(2, 1, head_width, width))
        if layer + 1 < LAYERS:
            gathered = made[2]
        edges_out.append(
            jnp.einsum(
                "rp,pkc->rkc", choice, edge_sum[:9].reshape(PROMPTS, CONV - 1, width), precision=lax.Precision.HIGHEST
            ).astype(jnp.bfloat16)
        )
    return (current, jnp.stack(states), jnp.stack(edges_out))


def solution(mesh):
    return jax.shard_map(
        body,
        mesh=mesh,
        in_specs=(
            P("seq", ("wr", "wc")),
            P(),
            P(None, None, ("wr", "wc")),
            P(None, None, ("wr", "wc")),
            P(),
            P(),
            P(None, None, ("wr", "wc")),
            P(None, ("wr", "wc")),
            P(None, "wr", None, None, None),
            P(None, "wr", None, None, None),
            P(None, "wr", None, "wc", None),
            P(None, ("wr", "wc")),
            P(None, ("wr", "wc")),
            P(None, ("wr", "wc"), None),
            P(),
            P("seq"),
        ),
        out_specs=(
            P("seq", ("wr", "wc")),
            P(None, "seq", "wr", None, "wc"),
            P(None, "seq", None, ("wr", "wc")),
        ),
        check_vma=False,
    )
```

time: 1100 us -> 356 us (0.32)
  waiting for transfers between devices: 757 us -> 0 us
  Pallas kernels: 0 us -> 245 us
  blocking collectives: 125 us -> 6.73 us
  local copies, waits for them, and re-layouts: 79.5 us -> 33.2 us
  matrix products: 59.7 us -> 28.6 us
  between operations: 24.4 us -> 9.79 us
    all_gather x8 -> x0, waiting for transfers between devices: 390 us -> none  [the longest x2 233 us: entering_2(): lax.all_gather(a.astype(kind), axis)]
    pallas_call x0 -> x9, Pallas kernels: none -> 245 us  [the longest x2 111 us: scan_states(): pl.pallas_call(kernel, out_shape=(jax.ShapeDtypeStruct((spans, part, widt...]
    unnamed x13 -> x0, waiting for transfers between devices: 197 us -> none
    psum x1 -> x0, waiting for transfers between devices: 169 us -> none  [broadcast(): return lax.psum(jnp.where(mine, shard, jnp.zeros_like(shard)), axis)]
    unnamed x2 -> x0, blocking collectives: 106 us -> none
    dot_general x22 -> x12, matrix products: 54.3 us -> 26.2 us  [the longest x2 10.3 us: body(): jnp.dot(gated, w_down[layer], preferred_element_type=jnp.float32)]
    unnamed x126 -> x193, local copies, waits for them, and re-layouts: 27.7 us -> 4.29 us
    psum x2 -> x0, blocking collectives: 18.8 us -> none  [body(): lax.psum((jnp.sum(hidden_parts, axis=1), jnp.sum(hidden_parts * hidden_pa...]
  transfers between devices with their start and end apart: 13 -> 0, of which waited for: 12 -> 0; matrix products, arithmetic and copies ran while one was open for 8% -> 0% of each run, Pallas kernels for 0% -> 0%
where the time goes in v1:
time: 356 us; the launch traced here: 354 us
  Pallas kernels  245 us (69%)
  local copies, waits for them, and re-layouts  33.2 us (9%)
  other arithmetic  30.6 us (9%)
  matrix products  28.6 us (8%)
  between operations  9.79 us (3%)
  blocking collectives  6.73 us (2%)
    pallas_call x2, Pallas kernels, scan_states(): pl.pallas_call(kernel, out_shape=(jax.ShapeDtypeStruct((spans, part, widt...  111 us
    pallas_call x2, Pallas kernels, reduce_plane(): pl.pallas_call(kernel, out_shape=tuple(shapes), in_specs=[VM] * 3, out_sp...  80.3 us
    pallas_call x2, Pallas kernels, gather_head(): pl.pallas_call(kernel, out_shape=(jax.ShapeDtypeStruct((rows, width * 4),...  23.8 us
    pallas_call x1, Pallas kernels, gather16(): pl.pallas_call(kernel, out_shape=jax.ShapeDtypeStruct((rows, width * 16),...  18.8 us
    pallas_call x2, Pallas kernels, sum_wc(): pl.pallas_call(kernel, out_shape=jax.ShapeDtypeStruct(sums.shape, sums.dt...  10.8 us
    dot_general x2, matrix products, body(): jnp.dot(gated, w_down[layer], preferred_element_type=jnp.float32)  10.3 us
    reshape x2, local copies, waits for them, and re-layouts, body(): sums = sums.reshape(SEQ, head_width // SEQ, 3, width)  8.32 us

profile of v1, /device:TPU:8, one launch (start us, length us, event | category | flops | bytes accessed | tf_op | source)
XLA Modules:
  0.0 353.7 jit_solution(2981925210290548797)
XLA Ops:
  21.1 6.7 %all_gather.3 = f32[2,5,1024]{2,1,0:T(8,128)S(1)} all-gather(f32[2,5,256]{2,1,0:T(8,128)S(1)} %pad_maximum_fusion.11), channel_id=1, replica_groups=mesh['seq'=16,'wr'=4,'wc'=4] {'wc'}, dimensions={2}, use_global_device_ids=true | all-gather | bytes 51200 | tf_op jit(solution)/shard_map/all_gather | solution.py:469
  29.4 18.8 %gather_tokens.1 = bf16[512,2048]{1,0:T(8,128)(2,1)S(1)} custom-call(bf16[512,128]{1,0:T(8,128)(2,1)S(1)} %copy-done.2), custom_call_target="tpu_custom_call" | custom-call | tf_op jit(solution)/shard_map/gather_tokens/pallas_call | solution.py:100
  55.1 2.0 add_subtract_fusion.5
  60.3 11.8 %gather_head.2 = (bf16[512,1024]{1,0:T(8,128)(2,1)S(1)}, bf16[16,1024]{1,0:T(8,128)(2,1)S(1)}) custom-call(bf16[512,256]{1,0:T(8,128)(2,1)S(1)} %convolution_convert_fusion.5.own_ref), custom_call_target="tpu_custom_call" | custom-call | tf_op jit(solution)/shard_map/gather_head/pallas_call | solution.py:142
  73.4 2.8 fusion.174
  79.2 3.0 fusion.29
  82.2 2.2 convolution_convert_fusion.3
  84.4 4.2 %reshape.647 = bf16[16,64,3,256]{3,2,1,0:T(4,128)(2,1)S(1)} reshape(bf16[1024,768]{1,0:T(8,128)(2,1)} %convolution_convert_fusion.3) | data formatting | bytes 3145728 | tf_op jit(solution)/shard_map/reshape | solution.py:509
  88.5 2.3 fusion.176
  91.2 57.5 %scan_states.2 = (bf16[16,64,256]{2,1,0:T(8,128)(2,1)S(1)}, bf16[16,2,64,256]{3,2,1,0:T(8,128)(2,1)S(1)}, f32[16,256]{1,0:T(8,128)S(1)}) custom-call(bf16[16,64,256]{2,1,0:T(8,128)(2,1)S(1)} %bitcast.257, bf16[16,64,256]{2,1,0:T(8,128)(2,1)S(1)} %bitcast.255, bf16[16,64,256]{2,1,0:T(8,128)(2,1)S(1)} %bitcast.253, f32[24,256]{1,0:T(8,128)S(1)} %maximum_maximum_fusion.small_ref), custom_call_target="tpu_custom_call" | custom-call | tf_op jit(solution)/shard_map/scan_states/pallas_call | solution.py:258
  150.2 5.4 %sum_wc.2 = f32[8,512]{1,0:T(8,128)S(1)} custom-call(f32[8,512]{1,0:T(8,128)S(1)} %maximum_maximum_fusion.2.own_ref), custom_call_target="tpu_custom_call" | custom-call | tf_op jit(solution)/shard_map/sum_wc/pallas_call | solution.py:293
  155.7 5.5 %convolution_convert_fusion.1.refs_0_ = bf16[512,2048]{1,0:T(8,128)(2,1)} fusion(bf16[2,256,2048]{2,1,0:T(8,128)(2,1)} %param.29, bf16[512,2048]{1,0:T(8,128)(2,1)S(1)} %copy-done.6, bf16[2,2048,256]{2,1,0:T(8,128)(2,1)} %param.19, f32[512,256]{1,0:T(8,128)} %get-tuple-element.207, bf16[512,1024]{1,0:T(8,128)(2,1)} %get-tuple-element.57, ...), kind=kOutput, calls=%fused_computation.15 | convolution fusion | flops 1076363264 | bytes 7084036 | tf_op jit(solution)/shard_map/dot_general | solution.py:537
  161.4 47.3 %reduce_gather.1 = (bf16[512,128]{1,0:T(8,128)(2,1)S(1)}, bf16[2,16,64,256]{3,2,1,0:T(8,128)(2,1)S(1)}, bf16[512,2048]{1,0:T(8,128)(2,1)S(1)}) custom-call(bf16[512,2048]{1,0:T(8,128)(2,1)} %convolution_convert_fusion.1.refs_0_, bf16[512,128]{1,0:T(8,128)(2,1)S(1)} %copy-done.3, bf16[16,2,64,256]{3,2,1,0:T(8,128)(2,1)S(1)} %get-tuple-element.21.refs_2_), custom_call_target="tpu_custom_call" | custom-call | tf_op jit(solution)/shard_map/reduce_gather/pallas_call | solution.py:397
  217.7 1.9 convolution_convert_fusion.4.own_ref
  219.6 12.0 %gather_head.3 = (bf16[512,1024]{1,0:T(8,128)(2,1)S(1)}, bf16[16,1024]{1,0:T(8,128)(2,1)S(1)}) custom-call(bf16[512,256]{1,0:T(8,128)(2,1)S(1)} %convolution_convert_fusion.4.own_ref), custom_call_target="tpu_custom_call" | custom-call | tf_op jit(solution)/shard_map/gather_head/pallas_call | solution.py:142
  233.5 2.8 fusion.173
  240.2 3.0 fusion.28
  243.2 2.2 convolution_convert_fusion.2
  245.4 4.2 %reshape.650 = bf16[16,64,3,256]{3,2,1,0:T(4,128)(2,1)S(1)} reshape(bf16[1024,768]{1,0:T(8,128)(2,1)} %convolution_convert_fusion.2) | data formatting | bytes 3145728 | tf_op jit(solution)/shard_map/reshape | solution.py:509
  249.6 2.5 fusion.175
  252.5 53.6 %scan_states.3 = (bf16[16,64,256]{2,1,0:T(8,128)(2,1)S(1)}, bf16[16,2,64,256]{3,2,1,0:T(8,128)(2,1)S(1)}, f32[16,256]{1,0:T(8,128)S(1)}) custom-call(bf16[16,64,256]{2,1,0:T(8,128)(2,1)S(1)} %bitcast.258, bf16[16,64,256]{2,1,0:T(8,128)(2,1)S(1)} %bitcast.256, bf16[16,64,256]{2,1,0:T(8,128)(2,1)S(1)} %bitcast.254, f32[24,256]{1,0:T(8,128)S(1)} %maximum_maximum_fusion.1.small_ref), custom_call_target="tpu_custom_call" | custom-call | tf_op jit(solution)/shard_map/scan_states/pallas_call | solution.py:258
  307.5 5.4 %sum_wc.3 = f32[8,512]{1,0:T(8,128)S(1)} custom-call(f32[8,512]{1,0:T(8,128)S(1)} %maximum_maximum_fusion.3.own_ref), custom_call_target="tpu_custom_call" | custom-call | tf_op jit(solution)/shard_map/sum_wc/pallas_call | solution.py:293
  312.9 4.8 %convolution_convert_fusion.refs_0_ = bf16[512,2048]{1,0:T(8,128)(2,1)S(1)} fusion(bf16[2,256,2048]{2,1,0:T(8,128)(2,1)} %param.29, bf16[512,2048]{1,0:T(8,128)(2,1)} %copy-done.4, bf16[2,2048,256]{2,1,0:T(8,128)(2,1)} %param.19, f32[512,256]{1,0:T(8,128)} %get-tuple-element.208, bf16[512,1024]{1,0:T(8,128)(2,1)} %get-tuple-element.50, s32[]{:T(128)S(6)} %select_n.214, ...), kind=kOutput, calls=%fused_computation.14 | convolution fusion | flops 1076363264 | bytes 7084036 | tf_op jit(solution)/shard_map/dot_general | solution.py:537
  317.7 33.0 %reduce_last.1 = (bf16[512,128]{1,0:T(8,128)(2,1)S(1)}, bf16[2,16,64,256]{3,2,1,0:T(8,128)(2,1)S(1)}) custom-call(bf16[512,2048]{1,0:T(8,128)(2,1)S(1)} %convolution_convert_fusion.refs_0_, bf16[512,128]{1,0:T(8,128)(2,1)S(1)} %get-tuple-element.26.refs_1_, bf16[16,2,64,256]{3,2,1,0:T(8,128)(2,1)S(1)} %get-tuple-element.27.refs_2_), custom_call_target="tpu_custom_call" | custom-call | tf_op jit(solution)/shard_map/reduce_last/pallas_call | solution.py:397
  (293 shorter events, 49.1 us)
Async XLA Ops:
  0.7 49.7 %copy-start.75 = (f32[4]{0:T(128)}, f32[4]{0:T(128)S(1)}, u32[]{:S(2)}) copy-start(f32[4]{0:T(128)S(1)} %compare_convert_fusion.2) | copy-start | bytes 52
  0.7 54.3 %copy-start.79 = (f32[6]{0:T(128)}, f32[6]{0:T(128)S(1)}, u32[]{:S(2)}) copy-start(f32[6]{0:T(128)S(1)} %broadcast.651) | copy-start | bytes 76
  2.1 52.9 %copy-start.81 = (f32[6]{0:T(128)}, f32[6]{0:T(128)S(1)}, u32[]{:S(2)}) copy-start(f32[6]{0:T(128)S(1)} %reshape.654) | copy-start | bytes 76
  7.7 64.4 %copy-start.73 = (pred[3]{0:T(512)(128)(4,1)}, pred[3]{0:T(512)(128)(4,1)S(1)}, u32[]{:S(2)}) copy-start(pred[3]{0:T(512)(128)(4,1)S(1)} %compare_and_fusion.4) | copy-start | bytes 13
  8.9 63.2 %copy-start.25 = (pred[3]{0:T(512)(128)(4,1)}, pred[3]{0:T(512)(128)(4,1)S(1)}, u32[]{:S(2)}) copy-start(pred[3]{0:T(512)(128)(4,1)S(1)} %get-tuple-element.210) | copy-start | bytes 13
  8.9 63.2 %copy-start.27 = (pred[3]{0:T(512)(128)(4,1)}, pred[3]{0:T(512)(128)(4,1)S(1)}, u32[]{:S(2)}) copy-start(pred[3]{0:T(512)(128)(4,1)S(1)} %get-tuple-element.211) | copy-start | bytes 13
  9.5 69.7 %copy-start.23 = (s32[512]{0:T(512)}, s32[512]{0:T(512)S(1)}, u32[]{:S(2)}) copy-start(s32[512]{0:T(512)S(1)} %convert_add_fusion) | copy-start | bytes 6148
  14.8 58.6 %copy-start.16 = (f32[512]{0:T(512)}, f32[512]{0:T(512)S(1)}, u32[]{:S(2)}) copy-start(f32[512]{0:T(512)S(1)} %get-tuple-element.180) | copy-start | bytes 6148
  49.8 8.6 %copy-start.5 = (bf16[512,2048]{1,0:T(8,128)(2,1)}, bf16[512,2048]{1,0:T(8,128)(2,1)S(1)}, u32[]{:S(2)}) copy-start(bf16[512,2048]{1,0:T(8,128)(2,1)S(1)} %fusion.2) | copy-start | bytes 6291460
  90.9 57.8 %copy-start.9 = (bf16[512,256]{1,0:T(8,128)(2,1)S(1)}, bf16[512,256]{1,0:T(8,128)(2,1)}, u32[]{:S(2)}) copy-start(bf16[512,256]{1,0:T(8,128)(2,1)} %get-tuple-element.77) | copy-start | bytes 786436
  90.9 57.8 %copy-start.12 = (bf16[512,256]{1,0:T(8,128)(2,1)S(1)}, bf16[512,256]{1,0:T(8,128)(2,1)}, u32[]{:S(2)}) copy-start(bf16[512,256]{1,0:T(8,128)(2,1)} %get-tuple-element.78) | copy-start | bytes 786436
  91.0 57.8 %copy-start.13 = (bf16[512,256]{1,0:T(8,128)(2,1)S(1)}, bf16[512,256]{1,0:T(8,128)(2,1)}, u32[]{:S(2)}) copy-start(bf16[512,256]{1,0:T(8,128)(2,1)} %get-tuple-element.79) | copy-start | bytes 786436
  91.0 57.8 %copy-start.78 = (f32[512]{0:T(512)S(1)}, f32[512]{0:T(512)}, u32[]{:S(2)}) copy-start(f32[512]{0:T(512)} %get-tuple-element.51) | copy-start | bytes 6148
  91.0 57.8 %copy-start.92 = (f32[512,256]{1,0:T(8,128)S(1)}, f32[512,256]{1,0:T(8,128)}, u32[]{:S(2)}) copy-start(f32[512,256]{1,0:T(8,128)} %fusion.29) | copy-start | bytes 1572868
  210.3 7.3 %copy-start.4 = (bf16[512,2048]{1,0:T(8,128)(2,1)}, bf16[512,2048]{1,0:T(8,128)(2,1)S(1)}, u32[]{:S(2)}) copy-start(bf16[512,2048]{1,0:T(8,128)(2,1)S(1)} %fusion.6) | copy-start | bytes 6291460
  217.7 14.0 %copy-start.26 = (pred[3]{0:T(512)(128)(4,1)S(1)}, pred[3]{0:T(512)(128)(4,1)}, u32[]{:S(2)}) copy-start(pred[3]{0:T(512)(128)(4,1)} %copy-done.25) | copy-start | bytes 13
  217.7 14.0 %copy-start.28 = (pred[3]{0:T(512)(128)(4,1)S(1)}, pred[3]{0:T(512)(128)(4,1)}, u32[]{:S(2)}) copy-start(pred[3]{0:T(512)(128)(4,1)} %copy-done.27) | copy-start | bytes 13
  217.7 14.0 %copy-start.74 = (pred[3]{0:T(512)(128)(4,1)S(1)}, pred[3]{0:T(512)(128)(4,1)}, u32[]{:S(2)}) copy-start(pred[3]{0:T(512)(128)(4,1)} %copy-done.73) | copy-start | bytes 13
  252.2 53.9 %copy-start.7 = (bf16[512,256]{1,0:T(8,128)(2,1)S(1)}, bf16[512,256]{1,0:T(8,128)(2,1)}, u32[]{:S(2)}) copy-start(bf16[512,256]{1,0:T(8,128)(2,1)} %get-tuple-element.65) | copy-start | bytes 786436
  252.2 53.9 %copy-start.8 = (bf16[512,256]{1,0:T(8,128)(2,1)S(1)}, bf16[512,256]{1,0:T(8,128)(2,1)}, u32[]{:S(2)}) copy-start(bf16[512,256]{1,0:T(8,128)(2,1)} %get-tuple-element.66) | copy-start | bytes 786436
  252.2 53.9 %copy-start.10 = (bf16[512,256]{1,0:T(8,128)(2,1)S(1)}, bf16[512,256]{1,0:T(8,128)(2,1)}, u32[]{:S(2)}) copy-start(bf16[512,256]{1,0:T(8,128)(2,1)} %get-tuple-element.67) | copy-start | bytes 786436
  252.2 53.9 %copy-start.11 = (bf16[512,256]{1,0:T(8,128)(2,1)S(1)}, bf16[512,256]{1,0:T(8,128)(2,1)}, u32[]{:S(2)}) copy-start(bf16[512,256]{1,0:T(8,128)(2,1)} %get-tuple-element.68) | copy-start | bytes 786436
  252.3 53.9 %copy-start.91 = (f32[512,256]{1,0:T(8,128)S(1)}, f32[512,256]{1,0:T(8,128)}, u32[]{:S(2)}) copy-start(f32[512,256]{1,0:T(8,128)} %fusion.28) | copy-start | bytes 1572868
  317.7 33.0 %copy-start.1 = (bf16[2,16,64,256]{3,2,1,0:T(8,128)(2,1)S(1)}, bf16[2,16,64,256]{3,2,1,0:T(8,128)(2,1)}, u32[]{:S(2)}) copy-start(bf16[2,16,64,256]{3,2,1,0:T(8,128)(2,1)} %copy-done) | copy-start | bytes 3145732
  (69 other events, 134.0 us)

commit v2 on v1

--- a/solution.py
+++ b/solution.py
@@ -153,37 +153,107 @@
     )(branch)
 
 
-SMALL = 24
-
-
-def scan_states(grown, ends_a, ends_b, small):
-    spans, part, width = grown.shape
+def tail(sums, small, edges, lines, queries, keys, values, act, outgate, gains, w_down, current, gather):
+    spans, part, wide = sums.shape
+    cols = wide // 3
+    rows, width = current.shape
+    head_width = queries.shape[1]
+    tile = 128
+    tiles = rows // tile
 
     def kernel(
-        grown_ref, a_ref, b_ref, small_ref, state_ref, chosen_ref, edge_ref,
-        got, got_a, got_b, got_small, going, total, send, recv, local,
+        sums_ref, small_ref, edges_ref, lines_ref, q_ref, k_ref, v_ref, act_ref, og_ref, gains_ref, down_ref, cur_ref,
+        *refs,
     ):
+        new_ref, req_ref, edge_ref = refs[:3]
+        if gather:
+            out_ref, gsend, grecv = refs[3], refs[-2], refs[-1]
+            refs = refs[:3] + refs[4:-2]
+        (got, got_a, got_b, got_small, got_edges, going, state_ref, total, chosen, upright, hidden, stat, got_stat,
+         gated, term, near, held, far, last, pair, send, recv, esend, erecv, local) = refs[3:]
         place = lax.axis_index("seq")
+        row, col, core, cross, mate = plane()
         peers = [lax.rem(place + d, SEQ) for d in range(SEQ)]
-        greet([{"seq": peers[d]} for d in range(1, SEQ)])
-        sent = [[], [], [], []]
+        wc_peers = [{"wc": lax.rem(col + d, 4)} for d in (1, 2, 3)]
+        greet(
+            [{"wr": lax.rem(row + d, 4)} for d in (1, 2, 3)] + wc_peers + [{"seq": peers[d]} for d in range(1, SEQ)]
+        )
+        inc, end_a, end_b = [pl.ds(i * cols, cols) for i in range(3)]
+        sent = []
+        arrive = []
         for d in range(1, SEQ):
             to = {"seq": peers[d]}
-            sent[0].append(copy_to(small_ref, got_small.at[place], send.at[0, d], recv.at[0, d], to))
-            sent[1].append(copy_to(grown_ref.at[peers[d]], got.at[place], send.at[1, d], recv.at[1, d], to))
+            arrive.append(copy_to(small_ref, got_small.at[place], send.at[0, d], recv.at[0, d], to))
+            arrive.append(copy_to(sums_ref.at[peers[d], :, inc], got.at[place], send.at[1, d], recv.at[1, d], to))
+        sent += arrive
         own = [
             pltpu.make_async_copy(small_ref, got_small.at[place], local.at[0]),
-            pltpu.make_async_copy(grown_ref.at[place], got.at[place], local.at[1]),
-            pltpu.make_async_copy(a_ref.at[place], got_a.at[place], local.at[2]),
+            pltpu.make_async_copy(sums_ref.at[place, :, inc], got.at[place], local.at[1]),
+            pltpu.make_async_copy(sums_ref.at[place, :, end_a], got_a.at[place], local.at[2]),
+            pltpu.make_async_copy(edges_ref, got_edges.at[place], local.at[3]),
         ]
         for made in own:
             made.start()
+
+        upright[...] = jnp.transpose(
+            jnp.concatenate([lines_ref[...], jnp.zeros((128 - lines_ref.shape[0], rows), jnp.float32)])
+        )
+        for r in range(tiles):
+            at = pl.ds(r * tile, tile)
+            seen = (r + 1) * tile
+            scores = lax.dot_general(
+                q_ref[at], k_ref[pl.ds(0, seen)], FEATURE_DIMS, preferred_element_type=jnp.float32
+            )
+            gap = upright[at, 0:1] - lines_ref[0:1, 0:seen] + lines_ref[1:2, 0:seen]
+            early = (
+                lax.broadcasted_iota(jnp.int32, (tile, seen), 0) + r * tile
+                >= lax.broadcasted_iota(jnp.int32, (tile, seen), 1)
+            )
+            allowed = early & (upright[at, 2:3] == lines_ref[2:3, 0:seen])
+            scores = scores * jnp.exp(jnp.where(allowed, gap, -jnp.inf))
+            hidden[at] = jnp.dot(
+                scores.astype(jnp.bfloat16), v_ref[pl.ds(0, seen)], preferred_element_type=jnp.float32
+            )
+
+        for made in own:
+            made.wait()
+        for made in arrive:
+            made.wait_recv()
+
+        def scalar(k, i):
+            line = got_small[k, i : i + 1]
+            return jnp.concatenate([line] * (cols // 128), axis=1)
+
+        state = jnp.zeros((part, cols), jnp.float32)
+        first = jnp.zeros((part, cols), jnp.float32)
+        second = jnp.zeros((part, cols), jnp.float32)
+        for k in range(SEQ):
+            going[k] = state.astype(jnp.bfloat16)
+            if k <= SPLIT:
+                first = first + scalar(k, 1) * state
+            if k >= SPLIT:
+                second = second + scalar(k, 2) * state
+            state = scalar(k, 0) * state + got[k].astype(jnp.float32)
+        total[0] = first
+        total[1] = second
+        total[2] = state
+        arrive = [
+            copy_to(going.at[peers[d]], state_ref.at[place], send.at[3, d], recv.at[3, d], {"seq": peers[d]})
+            for d in range(1, SEQ)
+        ]
+        sent += arrive
+        state_ref[place] = going[place]
+        for made in arrive:
+            made.wait_recv()
+        late = []
         for d in range(1, SEQ):
             to = {"seq": peers[d]}
-            sent[2].append(copy_to(a_ref.at[peers[d]], got_a.at[place], send.at[2, d], recv.at[2, d], to))
+            late.append(copy_to(edges_ref, got_edges.at[place], send.at[5, d], recv.at[5, d], to))
+            late.append(copy_to(sums_ref.at[peers[d], :, end_a], got_a.at[place], send.at[2, d], recv.at[2, d], to))
+        sent += late
         b_copies = [
             pltpu.make_async_remote_copy(
-                src_ref=b_ref.at[peers[d]], dst_ref=got_b, send_sem=send.at[4, d], recv_sem=recv.at[4, 0],
+                src_ref=sums_ref.at[peers[d], :, end_b], dst_ref=got_b, send_sem=send.at[4, d], recv_sem=recv.at[4, 0],
                 device_id={"seq": peers[d]}, device_id_type=MESH,
             )
             for d in range(1, SEQ)
@@ -193,167 +263,106 @@
         def _():
             for made in b_copies:
                 made.start()
-            made = pltpu.make_async_copy(b_ref.at[place], got_b, local.at[3])
+            made = pltpu.make_async_copy(sums_ref.at[place, :, end_b], got_b, local.at[4])
             made.start()
             made.wait()
 
-        for made in own:
-            made.wait()
-        for made in sent[0] + sent[1]:
+        lane = lax.broadcasted_iota(jnp.int32, (tile, 128), 1)
+        whole = state_ref[...].reshape(head_width, cols)
+        for r in range(tiles):
+            at = pl.ds(r * tile, tile)
+            here = hidden[at] + upright[at, 3:4] * jnp.dot(q_ref[at], whole, preferred_element_type=jnp.float32)
+            hidden[at] = here
+            ones = jnp.sum(here, axis=1, keepdims=True)
+            twos = jnp.sum(here * here, axis=1, keepdims=True)
+            upright[at] = jnp.where(lane == 0, ones, jnp.where(lane == 1, twos, 0.0))
+        stat[...] = jnp.transpose(upright[...])[0:8]
+        arrive = [copy_to(stat, got_stat.at[d], esend.at[d], erecv.at[d], wc_peers[d]) for d in range(3)]
+        sent += arrive
+        for made in arrive:
             made.wait_recv()
-        state = jnp.zeros((part, width), jnp.float32)
-        first = jnp.zeros((part, width), jnp.float32)
-        second = jnp.zeros((part, width), jnp.float32)
-        for k in range(SEQ):
-            going[k] = state.astype(jnp.bfloat16)
-            if k <= SPLIT:
-                first = first + got_small[k, 10:11] * state
-            if k >= SPLIT:
-                second = second + got_small[k, 11:12] * state
-            state = got_small[k, 9:10] * state + got[k].astype(jnp.float32)
-        total[0] = first
-        total[1] = second
-        total[2] = state
-        for d in range(1, SEQ):
-            sent[3].append(
-                copy_to(going.at[peers[d]], state_ref.at[place], send.at[3, d], recv.at[3, d], {"seq": peers[d]})
-            )
-        state_ref[place] = going[place]
-        edge = got_small[0, 0:16]
-        for k in range(1, SEQ):
-            edge = edge + got_small[k, 0:16]
-        edge_ref[...] = edge
-        for made in sent[2]:
-            made.wait_recv()
-
-        @pl.when(place != SPLIT)
-        def _():
-            b_copies[0].wait_recv()
-
-        first, second, third = total[0], total[1] + got_b[...].astype(jnp.float32), total[2]
-        for k in range(SEQ):
-            if k <= SPLIT:
-                first = first + got_a[k].astype(jnp.float32)
-            else:
-                second = second + got_a[k].astype(jnp.float32)
-        for k in range(SEQ):
-            for j in range(2):
-                row = 12 + 3 * j
-                chosen_ref[k, j] = (
-                    got_small[k, row : row + 1] * first
-                    + got_small[k, row + 1 : row + 2] * second
-                    + got_small[k, row + 2 : row + 3] * third
-                ).astype(jnp.bfloat16)
-        for made in sent[3]:
-            made.wait_recv()
-        for group in sent:
-            for made in group:
-                made.wait_send()
-
-        @pl.when(place == SPLIT)
-        def _():
-            for made in b_copies:
-                made.wait_send()
-
-    return pl.pallas_call(
-        kernel,
-        out_shape=(
-            jax.ShapeDtypeStruct((spans, part, width), jnp.bfloat16),
-            jax.ShapeDtypeStruct((spans, 2, part, width), jnp.bfloat16),
-            jax.ShapeDtypeStruct((16, width), jnp.float32),
-        ),
-        in_specs=[VM] * 4,
-        out_specs=(VM, VM, VM),
-        scratch_shapes=[
-            pltpu.VMEM((spans, part, width), jnp.bfloat16),
-            pltpu.VMEM((spans, part, width), jnp.bfloat16),
-            pltpu.VMEM((part, width), jnp.bfloat16),
-            pltpu.VMEM((spans, SMALL, width), jnp.float32),
-            pltpu.VMEM((spans, part, width), jnp.bfloat16),
-            pltpu.VMEM((3, part, width), jnp.float32),
-            DMA((5, SEQ)),
-            DMA((5, SEQ)),
-            DMA((4,)),
-        ],
-        compiler_params=params(3),
-        name="scan_states",
-    )(grown, ends_a, ends_b, small)
-
-
-def sum_wc(sums):
-    def kernel(own_ref, out_ref, got, send, recv):
-        col = lax.axis_index("wc")
-        peers = [{"wc": lax.rem(col + d, 4)} for d in (1, 2, 3)]
-        greet(peers)
-        sent = [copy_to(own_ref, got.at[d], send.at[d], recv.at[d], peers[d]) for d in range(3)]
-        for made in sent:
-            made.wait()
-        out_ref[...] = own_ref[...] + got[0] + got[1] + got[2]
-
-    return pl.pallas_call(
-        kernel,
-        out_shape=jax.ShapeDtypeStruct(sums.shape, sums.dtype),
-        in_specs=[VM],
-        out_specs=VM,
-        scratch_shapes=[pltpu.VMEM((3,) + sums.shape, sums.dtype), DMA((3,)), DMA((3,))],
-        compiler_params=params(4),
-        name="sum_wc",
-    )(sums)
-
-
-def reduce_plane(terms, current, chosen, gather):
-    rows, width = current.shape
-    spans, reqs, part, cols = chosen.shape
-
-    def kernel(*refs):
-        if gather:
-            (term_ref, cur_ref, chosen_ref, new_ref, req_ref, out_ref, near, held, far, last, pair,
-             send, recv, fsend, frecv, local, gsend, grecv) = refs
-        else:
-            (term_ref, cur_ref, chosen_ref, new_ref, req_ref, near, held, far, last, pair,
-             send, recv, fsend, frecv, local) = refs
-        place = lax.axis_index("seq")
-        row, col, core, cross, mate = plane()
-        spans_to = [lax.rem(place + d, SEQ) for d in range(SEQ)]
-        greet(plane_peers(row, cross, mate) + [{"seq": spans_to[d]} for d in range(1, SEQ)])
+        sums_all = stat[...] + got_stat[0] + got_stat[1] + got_stat[2]
+        upright[...] = jnp.transpose(jnp.concatenate([sums_all, jnp.zeros((120, rows), jnp.float32)]))
+        for r in range(tiles):
+            at = pl.ds(r * tile, tile)
+            mean = upright[at, 0:1] / head_width
+            var = upright[at, 1:2] / head_width - mean * mean
+            normal = (hidden[at] - mean) * lax.rsqrt(var + EPSILON)
+            gate = og_ref[at]
+            gated[at] = (
+                (normal * gains_ref[0:1] + gains_ref[1:2] * act_ref[at].astype(jnp.float32)) * (gate * jax.nn.sigmoid(gate))
+            ).astype(jnp.bfloat16)
+
         order = [2, 1, 3, 0]
         rows_to = [lax.rem(row + d, 4) for d in range(4)]
-
-        def block(r, c):
-            return pl.ds(pl.multiple_of((r * 4 + c) * width, width), width)
-
         first = []
-        for i, d in enumerate(order):
+        for d in order:
+            term[d] = jnp.dot(
+                gated[...], down_ref[:, pl.ds(pl.multiple_of(rows_to[d] * 4 * width, 4 * width), 4 * width)],
+                preferred_element_type=jnp.float32,
+            ).astype(jnp.bfloat16)
             for h in range(2):
                 first.append(
                     copy_to(
-                        term_ref.at[:, block(rows_to[d], 2 * h + 1 - core)], near.at[2 * d + h],
-                        send.at[2 * d + h], recv.at[2 * d + h], {"wc": mate},
+                        term.at[d, :, pl.ds(pl.multiple_of((2 * h + 1 - core) * width, width), width)],
+                        near.at[2 * d + h], send.at[6, 2 * d + h], recv.at[6, 2 * d + h], {"wc": mate},
                     )
                 )
-        side = [
-            copy_to(chosen_ref.at[spans_to[d]], req_ref.at[:, place], fsend.at[d], frecv.at[d], {"seq": spans_to[d]})
-            for d in range(1, SEQ)
-        ]
-        keep = pltpu.make_async_copy(chosen_ref.at[place], req_ref.at[:, place], local)
-        keep.start()
         second = []
         for i, d in enumerate(order):
             for h in range(2):
                 first[2 * i + h].wait_recv()
-                total = term_ref[:, block(rows_to[d], 2 * h + core)].astype(jnp.float32) + near[2 * d + h].astype(
-                    jnp.float32
-                )
+                block = term[d, :, pl.ds(pl.multiple_of((2 * h + core) * width, width), width)]
+                whole = block.astype(jnp.float32) + near[2 * d + h].astype(jnp.float32)
                 if d > 0:
-                    held[2 * d + h] = total.astype(jnp.bfloat16)
+                    held[2 * d + h] = whole.astype(jnp.bfloat16)
                 else:
-                    pair[h] = total
+                    pair[h] = whole
             if d > 0:
                 second.append(
-                    copy_to(
-                        held.at[pl.ds(2 * d, 2)], far.at[d - 1], send.at[8 + d], recv.at[8 + d], {"wr": rows_to[d]}
-                    )
+                    copy_to(held.at[pl.ds(2 * d, 2)], far.at[d - 1], esend.at[4 + d], erecv.at[4 + d], {"wr": rows_to[d]})
                 )
+        sent += first + second
+
+        for made in late:
+            made.wait_recv()
+
+        @pl.when(place != SPLIT)
+        def _():
+            b_copies[0].wait_recv()
+
+        first, second_end, third = total[0], total[1] + got_b[...].astype(jnp.float32), total[2]
+        edge = jnp.zeros((16, cols), jnp.float32)
+        for k in range(SEQ):
+            edge = edge + got_edges[k].astype(jnp.float32)
+            if k <= SPLIT:
+                first = first + got_a[k].astype(jnp.float32)
+            else:
+                second_end = second_end + got_a[k].astype(jnp.float32)
+        total[0] = first
+        total[1] = second_end
+        side = []
+        for d in range(1, SEQ):
+            for j in range(2):
+                which = got_small[peers[d], 3 + j : 4 + j]
+                which = jnp.concatenate([which] * (cols // 128), axis=1)
+                chosen[peers[d], j] = jnp.where(
+                    which == 0.0, total[0], jnp.where(which == 1.0, total[1], total[2])
+                ).astype(jnp.bfloat16)
+            side.append(
+                copy_to(chosen.at[peers[d]], req_ref.at[:, place], send.at[7, d], recv.at[7, d], {"seq": peers[d]})
+            )
+        for j in range(2):
+            which = small_ref[3 + j : 4 + j]
+            which = jnp.concatenate([which] * (cols // 128), axis=1)
+            req_ref[j, place] = jnp.where(
+                which == 0.0, total[0], jnp.where(which == 1.0, total[1], total[2])
+            ).astype(jnp.bfloat16)
+            edge_ref[j, 0:3] = jnp.where(
+                which == 0.0, edge[0:3], jnp.where(which == 1.0, edge[3:6], edge[6:9])
+            )
+        sent += side
+
         for made in second:
             made.wait_recv()
         other = lax.rem(lax.div(col, 2) + 1, 2)
@@ -365,44 +374,66 @@
                 + far[2, h].astype(jnp.float32)
             )
         held[0] = pair[other].astype(jnp.bfloat16)
-        third = copy_to(held.at[0], last, send.at[8], recv.at[8], {"wc": cross})
-        third.wait_recv()
+        final = copy_to(held.at[0], last, esend.at[4], erecv.at[4], {"wc": cross})
+        sent.append(final)
+        final.wait_recv()
         new_ref[...] = (
             cur_ref[...].astype(jnp.float32) + (pair[1 - other] + last[...].astype(jnp.float32))
         ).astype(jnp.bfloat16)
         if gather:
-            out_ref[:, block(row, col)] = new_ref[...]
+            out_ref[:, pl.ds(pl.multiple_of((row * 4 + col) * width, width), width)] = new_ref[...]
             gather_plane(new_ref, out_ref, gsend, grecv)
         for made in side:
             made.wait_recv()
-        keep.wait()
-        for made in first + second + [third] + side:
+        for made in sent:
             made.wait_send()
 
+        @pl.when(place == SPLIT)
+        def _():
+            for made in b_copies:
+                made.wait_send()
+
+    b16, f32 = jnp.bfloat16, jnp.float32
     shapes = [
-        jax.ShapeDtypeStruct((rows, width), jnp.bfloat16),
-        jax.ShapeDtypeStruct((reqs, spans, part, cols), jnp.bfloat16),
+        jax.ShapeDtypeStruct((rows, width), b16),
+        jax.ShapeDtypeStruct((2, spans, part, cols), b16),
+        jax.ShapeDtypeStruct((2, 8, cols), f32),
     ]
     scratch = [
-        pltpu.VMEM((8, rows, width), jnp.bfloat16),
-        pltpu.VMEM((8, rows, width), jnp.bfloat16),
-        pltpu.VMEM((3, 2, rows, width), jnp.bfloat16),
-        pltpu.VMEM((rows, width), jnp.bfloat16),
-        pltpu.VMEM((2, rows, width), jnp.float32),
-        DMA((12,)), DMA((12,)), DMA((SEQ,)), DMA((SEQ,)), DMA,
+        pltpu.VMEM((spans, part, cols), b16),
+        pltpu.VMEM((spans, part, cols), b16),
+        pltpu.VMEM((part, cols), b16),
+        pltpu.VMEM((spans, 8, 128), f32),
+        pltpu.VMEM((spans, 16, cols), b16),
+        pltpu.VMEM((spans, part, cols), b16),
+        pltpu.VMEM((spans, part, cols), b16),
+        pltpu.VMEM((3, part, cols), f32),
+        pltpu.VMEM((spans, 2, part, cols), b16),
+        pltpu.VMEM((rows, 128), f32),
+        pltpu.VMEM((rows, cols), f32),
+        pltpu.VMEM((8, rows), f32),
+        pltpu.VMEM((3, 8, rows), f32),
+        pltpu.VMEM((rows, cols), b16),
+        pltpu.VMEM((4, rows, 4 * width), b16),
+        pltpu.VMEM((8, rows, width), b16),
+        pltpu.VMEM((8, rows, width), b16),
+        pltpu.VMEM((3, 2, rows, width), b16),
+        pltpu.VMEM((rows, width), b16),
+        pltpu.VMEM((2, rows, width), f32),
+        DMA((8, SEQ)), DMA((8, SEQ)), DMA((8,)), DMA((8,)), DMA((5,)),
     ]
     if gather:
-        shapes.append(jax.ShapeDtypeStruct((rows, width * 16), jnp.bfloat16))
+        shapes.append(jax.ShapeDtypeStruct((rows, width * 16), b16))
         scratch += [DMA((15,)), DMA((15,))]
     return pl.pallas_call(
         kernel,
         out_shape=tuple(shapes),
-        in_specs=[VM] * 3,
+        in_specs=[VM] * 12,
         out_specs=(VM,) * len(shapes),
         scratch_shapes=scratch,
         compiler_params=params(5 if gather else 6),
-        name="reduce_gather" if gather else "reduce_last",
-    )(terms, current, chosen)
+        name="tail_gather" if gather else "tail_last",
+    )(sums, small, edges, lines, queries, keys, values, act, outgate, gains, w_down, current)
 
 
 def norm_rows(source, gain_row):
@@ -463,8 +494,6 @@
     local_ends = [jnp.clip(end - row_offset, 0, tok_rows - 1) for end in ends]
     head_mask = (jnp.arange(HEADS, dtype=jnp.int32) == head_idx).astype(jnp.float32)
     row_order = jnp.arange(tok_rows)
-    allowed = (row_order[:, None] >= row_order[None, :]) & (segment[:, None] == segment[None, :])
-    choice = (request_prompt[:, None] == jnp.arange(PROMPTS, dtype=jnp.int32)[None, :]).astype(jnp.float32)
     conv_all = jnp.concatenate([conv_weight, conv_bias[:, None]], axis=1)
     conv_all = lax.all_gather(conv_all, "wc", axis=2, tiled=True)
     current = tokens
@@ -506,45 +535,34 @@
         sums = lax.dot_general(
             key_rows, weighted.reshape(tok_rows, -1), ROW_DIMS, preferred_element_type=jnp.float32
         ).astype(jnp.bfloat16)
-        sums = sums.reshape(SEQ, head_width // SEQ, 3, width)
+        sums = sums.reshape(SEQ, head_width // SEQ, 3 * width)
         own_extended = lax.dynamic_slice_in_dim(extended, col_idx * width, width, 1)
-        small_rows = []
+        edge_rows = []
         for prompt in range(PROMPTS):
             window = lax.dynamic_slice_in_dim(own_extended, local_ends[prompt] + 1, CONV - 1, 0)
             edge_pos = ends[prompt] - (CONV - 2) + jnp.arange(CONV - 1, dtype=jnp.int32)
             keep = (edge_pos >= starts[prompt]) & holders[prompt]
-            small_rows.append(jnp.where(keep[:, None], window.astype(jnp.float32), 0.0))
-        scalars = jnp.concatenate([jnp.stack([decay] + end_decays), choice.reshape(-1), jnp.zeros((SMALL - 18,))])
-        small = jnp.concatenate(small_rows + [jnp.broadcast_to(scalars[:, None], (scalars.shape[0], width))], axis=0)
-        scores = lax.dot_general(queries, key_rows, FEATURE_DIMS, preferred_element_type=jnp.float32) * jnp.exp(
-            jnp.where(allowed, cum_log[:, None] - cum_log[None, :] + in_gate[None, :], -jnp.inf)
+            edge_rows.append(jnp.where(keep[:, None], window, jnp.zeros_like(window)))
+        edges = jnp.concatenate(edge_rows + [jnp.zeros((7, width), jnp.bfloat16)], axis=0)
+        scalars = jnp.concatenate(
+            [jnp.stack([decay] + end_decays), request_prompt.astype(jnp.float32), jnp.zeros((3,), jnp.float32)]
         )
-        in_block = jnp.dot(scores.astype(jnp.bfloat16), values, preferred_element_type=jnp.float32)
+        small = jnp.broadcast_to(scalars[:, None], (8, 128))
         carried = jnp.where(segment == seg_before, jnp.exp(cum_log), 0.0)
-        state, chosen_states, edge_sum = scan_states(sums[:, :, 0], sums[:, :, 1], sums[:, :, 2], small)
-        state_here = state.reshape(head_width, width)
-        hidden = in_block + carried[:, None] * jnp.dot(queries, state_here, preferred_element_type=jnp.float32)
-        stats = jnp.stack([jnp.sum(hidden, axis=1), jnp.sum(hidden * hidden, axis=1)])
-        stats = sum_wc(jnp.concatenate([stats, jnp.zeros((6, tok_rows), jnp.float32)]))
-        row_mean = stats[0] / head_width
-        row_var = stats[1] / head_width - row_mean * row_mean
-        normal_rows = (hidden - row_mean[:, None]) * lax.rsqrt(row_var + EPSILON)[:, None]
+        lines = jnp.stack(
+            [cum_log, in_gate, segment.astype(jnp.float32), carried] + [jnp.zeros((tok_rows,), jnp.float32)] * 4
+        )
         conv_act = lax.dynamic_slice_in_dim(head_act, col_idx * width, width, 1)
-        gated = (
-            (normal_rows * norm_gain[layer] + skip_gain[layer] * conv_act.astype(jnp.float32))
-            * jax.nn.silu(outgate)
-        ).astype(jnp.bfloat16)
-        terms = jnp.dot(gated, w_down[layer], preferred_element_type=jnp.float32).astype(jnp.bfloat16)
-        made = reduce_plane(terms, current, chosen_states, layer + 1 < LAYERS)
+        gains = jnp.stack([norm_gain[layer], skip_gain[layer]])
+        made = tail(
+            sums, small, edges, lines, queries, key_rows, values, conv_act, outgate, gains, w_down[layer], current,
+            layer + 1 < LAYERS,
+        )
         current = made[0]
         states.append(made[1].reshape(2, 1, head_width, width))
+        edges_out.append(made[2][:, : CONV - 1].astype(jnp.bfloat16))
         if layer + 1 < LAYERS:
-            gathered = made[2]
-        edges_out.append(
-            jnp.einsum(
-                "rp,pkc->rkc", choice, edge_sum[:9].reshape(PROMPTS, CONV - 1, width), precision=lax.Precision.HIGHEST
-            ).astype(jnp.bfloat16)
-        )
+            gathered = made[3]
     return (current, jnp.stack(states), jnp.stack(edges_out))
 
 

time: 356 us -> 306 us (0.86)
  Pallas kernels: 245 us -> 215 us
  matrix products: 28.6 us -> 14.2 us
  local copies, waits for them, and re-layouts: 33.2 us -> 23.4 us
    pallas_call x6 -> x2, Pallas kernels: 202 us -> 173 us  [tail(): pl.pallas_call(kernel, out_shape=tuple(shapes), in_specs=[VM] * 12, out_s...]
    dot_general x8 -> x2, matrix products: 19.1 us -> 3.08 us  [body(): jnp.dot(normed, w_outgate[layer], preferred_element_type=jnp.float32)]
    reshape x4 -> x0, local copies, waits for them, and re-layouts: 8.34 us -> none  [the longest x2 8.32 us: body(): sums = sums.reshape(SEQ, head_width // SEQ, 3, width)]
    slice x5 -> x3, local copies, waits for them, and re-layouts: 7.55 us -> 1.6 us  [the longest x2 1.52 us: body(): gains = jnp.stack([norm_gain[layer], skip_gain[layer]])]
    unnamed x193 -> x154, local copies, waits for them, and re-layouts: 4.29 us -> 7.64 us
where the time goes in v2:
time: 306 us; the launch traced here: 302 us
  Pallas kernels  215 us (70%)
  other arithmetic  32.9 us (11%)
  local copies, waits for them, and re-layouts  23.4 us (8%)
  matrix products  14.2 us (5%)
  between operations  9.75 us (3%)
  blocking collectives  6.75 us (2%)
    pallas_call x2, Pallas kernels, tail(): pl.pallas_call(kernel, out_shape=tuple(shapes), in_specs=[VM] * 12, out_s...  173 us
    pallas_call x2, Pallas kernels, gather_head(): pl.pallas_call(kernel, out_shape=(jax.ShapeDtypeStruct((rows, width * 4),...  23.3 us
    pallas_call x1, Pallas kernels, gather16(): pl.pallas_call(kernel, out_shape=jax.ShapeDtypeStruct((rows, width * 16),...  18.8 us
    unnamed x154, local copies, waits for them, and re-layouts  7.64 us
    all_gather x1, blocking collectives, body(): conv_all = lax.all_gather(conv_all, 'wc', axis=2, tiled=True)  6.75 us

profile of v2, /device:TPU:8, one launch (start us, length us, event | category | flops | bytes accessed | tf_op | source)
XLA Modules:
  0.0 301.9 jit_solution(6859716206218376485)
XLA Ops:
  2.2 1.3 fusion.96
  14.1 1.4 fusion.91
  19.8 6.8 %all_gather.3 = f32[2,5,1024]{2,1,0:T(8,128)S(1)} all-gather(f32[2,5,256]{2,1,0:T(8,128)S(1)} %pad_maximum_fusion.5), channel_id=1, replica_groups=mesh['seq'=16,'wr'=4,'wc'=4] {'wc'}, dimensions={2}, use_global_device_ids=true | all-gather | bytes 51200 | tf_op jit(solution)/shard_map/all_gather | solution.py:498
  28.1 18.8 %gather_tokens.1 = bf16[512,2048]{1,0:T(8,128)(2,1)S(1)} custom-call(bf16[512,128]{1,0:T(8,128)(2,1)S(1)} %copy-done.2), custom_call_target="tpu_custom_call" | custom-call | tf_op jit(solution)/shard_map/gather_tokens/pallas_call | solution.py:100
  48.3 1.3 copy-done.12
  54.5 2.0 broadcast_subtract_fusion.5
  56.5 1.3 broadcast_select_fusion.1
  58.5 2.7 convolution_convert_fusion.3.own_ref
  61.7 1.5 fusion.29.og_ref
  63.2 11.6 %gather_head.2 = (bf16[512,1024]{1,0:T(8,128)(2,1)S(1)}, bf16[16,1024]{1,0:T(8,128)(2,1)S(1)}) custom-call(bf16[512,256]{1,0:T(8,128)(2,1)S(1)} %convolution_convert_fusion.3.own_ref), custom_call_target="tpu_custom_call" | custom-call | tf_op jit(solution)/shard_map/gather_head/pallas_call | solution.py:142
  76.7 2.0 fusion.84
  80.3 2.2 convolution_convert_fusion.1
  83.5 90.9 %tail_gather.1 = (bf16[512,128]{1,0:T(8,128)(2,1)S(1)}, bf16[2,16,64,256]{3,2,1,0:T(8,128)(2,1)S(1)}, f32[2,8,256]{2,1,0:T(8,128)S(1)}, bf16[512,2048]{1,0:T(8,128)(2,1)}) custom-call(bf16[16,64,768]{2,1,0:T(8,128)(2,1)} %bitcast.208, f32[8,128]{1,0:T(8,128)S(1)} %copy-done.7, bf16[16,256]{1,0:T(8,128)(2,1)S(1)} %copy-done.5, f32[8,512]{1,0:T(8,128)S(1)} %stack.66.lines_ref, ...), custom_call_target="tpu_custom_call" | custom-call | tf_op jit(solution)/shard_map/tail_gather/pallas_call | solution.py:428
  175.1 2.3 convert_reduce_fusion
  178.2 1.3 copy-done.10
  184.3 2.0 broadcast_subtract_fusion.2
  186.3 1.3 broadcast_select_fusion
  188.9 2.7 convolution_convert_fusion.2.own_ref
  192.1 1.5 fusion.26.og_ref
  193.6 11.7 %gather_head.3 = (bf16[512,1024]{1,0:T(8,128)(2,1)S(1)}, bf16[16,1024]{1,0:T(8,128)(2,1)S(1)}) custom-call(bf16[512,256]{1,0:T(8,128)(2,1)S(1)} %convolution_convert_fusion.2.own_ref), custom_call_target="tpu_custom_call" | custom-call | tf_op jit(solution)/shard_map/gather_head/pallas_call | solution.py:142
  210.1 2.2 fusion.83
  215.0 2.2 convolution_convert_fusion
  217.2 81.9 %tail_last.1 = (bf16[512,128]{1,0:T(8,128)(2,1)S(1)}, bf16[2,16,64,256]{3,2,1,0:T(8,128)(2,1)S(1)}, f32[2,8,256]{2,1,0:T(8,128)S(1)}) custom-call(bf16[16,64,768]{2,1,0:T(8,128)(2,1)} %bitcast.209, f32[8,128]{1,0:T(8,128)S(1)} %copy-done.6, bf16[16,256]{1,0:T(8,128)(2,1)S(1)} %copy-done.4, f32[8,512]{1,0:T(8,128)S(1)} %stack.72.lines_ref, ...), custom_call_target="tpu_custom_call" | custom-call | tf_op jit(solution)/shard_map/tail_last/pallas_call | solution.py:428
  299.1 1.5 pad_maximum_fusion.2
  (251 shorter events, 37.6 us)
Async XLA Ops:
  1.4 73.6 %copy-start.72 = (bf16[16]{0:T(256)(128)(2,1)}, bf16[16]{0:T(256)(128)(2,1)S(1)}, u32[]{:S(2)}) copy-start(bf16[16]{0:T(256)(128)(2,1)S(1)} %pad.32.clone) | copy-start | bytes 100
  6.6 68.2 %copy-start.70 = (pred[3]{0:T(512)(128)(4,1)}, pred[3]{0:T(512)(128)(4,1)S(1)}, u32[]{:S(2)}) copy-start(pred[3]{0:T(512)(128)(4,1)S(1)} %compare_and_fusion.4) | copy-start | bytes 13
  7.9 67.0 %copy-start.30 = (pred[3]{0:T(512)(128)(4,1)}, pred[3]{0:T(512)(128)(4,1)S(1)}, u32[]{:S(2)}) copy-start(pred[3]{0:T(512)(128)(4,1)S(1)} %get-tuple-element.188) | copy-start | bytes 13
  7.9 67.0 %copy-start.32 = (pred[3]{0:T(512)(128)(4,1)}, pred[3]{0:T(512)(128)(4,1)S(1)}, u32[]{:S(2)}) copy-start(pred[3]{0:T(512)(128)(4,1)S(1)} %get-tuple-element.189) | copy-start | bytes 13
  12.0 64.8 %copy-start.18 = (f32[512]{0:T(512)}, f32[512]{0:T(512)S(1)}, u32[]{:S(2)}) copy-start(f32[512]{0:T(512)S(1)} %get-tuple-element.159) | copy-start | bytes 6148
  12.0 64.8 %copy-start.20 = (f32[512]{0:T(512)}, f32[512]{0:T(512)S(1)}, u32[]{:S(2)}) copy-start(f32[512]{0:T(512)S(1)} %get-tuple-element.160) | copy-start | bytes 6148
  12.0 64.8 %copy-start.22 = (f32[512]{0:T(512)}, f32[512]{0:T(512)S(1)}, u32[]{:S(2)}) copy-start(f32[512]{0:T(512)S(1)} %get-tuple-element.161) | copy-start | bytes 6148
  58.5 2.7 copy-start.13
  58.5 3.2 %copy-start.74 = (bf16[2,2048,256]{2,1,0:T(8,128)(2,1)S(1)}, bf16[2,2048,256]{2,1,0:T(8,128)(2,1)}, u32[]{:S(2)}) copy-start(bf16[2,2048,256]{2,1,0:T(8,128)(2,1)} %param.19) | copy-start | bytes 6291460
  174.5 3.0 copy-start.14
  188.9 2.7 copy-start.11
  188.9 3.2 %copy-start.75 = (bf16[2,2048,256]{2,1,0:T(8,128)(2,1)S(1)}, bf16[2,2048,256]{2,1,0:T(8,128)(2,1)}, u32[]{:S(2)}) copy-start(bf16[2,2048,256]{2,1,0:T(8,128)(2,1)} %param.19) | copy-start | bytes 6291460
  192.1 13.3 %copy-start.31 = (pred[3]{0:T(512)(128)(4,1)S(1)}, pred[3]{0:T(512)(128)(4,1)}, u32[]{:S(2)}) copy-start(pred[3]{0:T(512)(128)(4,1)} %copy-done.30) | copy-start | bytes 13
  192.1 13.3 %copy-start.33 = (pred[3]{0:T(512)(128)(4,1)S(1)}, pred[3]{0:T(512)(128)(4,1)}, u32[]{:S(2)}) copy-start(pred[3]{0:T(512)(128)(4,1)} %copy-done.32) | copy-start | bytes 13
  192.1 13.3 %copy-start.71 = (pred[3]{0:T(512)(128)(4,1)S(1)}, pred[3]{0:T(512)(128)(4,1)}, u32[]{:S(2)}) copy-start(pred[3]{0:T(512)(128)(4,1)} %copy-done.70) | copy-start | bytes 13
  192.1 13.5 %copy-start.73 = (bf16[16]{0:T(256)(128)(2,1)S(1)}, bf16[16]{0:T(256)(128)(2,1)}, u32[]{:S(2)}) copy-start(bf16[16]{0:T(256)(128)(2,1)} %copy-done.72) | copy-start | bytes 100
  210.0 2.4 copy-start.42
  210.0 2.4 copy-start.43
  210.0 2.4 copy-start.44
  210.0 2.4 copy-start.45
  210.0 2.4 copy-start.46
  210.0 2.4 copy-start.47
  210.1 2.4 copy-start.48
  210.1 2.4 copy-start.49
  (52 other events, 63.0 us)

commit v3 on v2

--- a/solution.py
+++ b/solution.py
@@ -48,10 +48,6 @@
     cross = lax.rem(col + 2, 4)
     mate = col + 1 - 2 * core
     return row, col, core, cross, mate
-
-
-def plane_peers(row, cross, mate):
-    return [{"wr": lax.rem(row + d, 4)} for d in (1, 2, 3)] + [{"wc": cross}, {"wc": mate}]
 
 
 def gather_plane(own_ref, out_ref, send, recv):
@@ -88,24 +84,36 @@
         sent[slot].wait_send()
 
 
-def gather16(own):
+def gather16(own, taps):
     rows, width = own.shape
-
-    def kernel(own_ref, out_ref, send, recv):
+    deep, share = taps.shape
+
+    def kernel(own_ref, taps_ref, out_ref, all_ref, send, recv, tsend, trecv):
         row, col, core, cross, mate = plane()
-        greet(plane_peers(row, cross, mate))
+        around = [{"wc": lax.rem(col + d, 4)} for d in (1, 2, 3)]
+        greet([{"wr": lax.rem(row + d, 4)} for d in (1, 2, 3)] + around)
+        mine = pl.ds(pl.multiple_of(col * share, share), share)
+        made = [copy_to(taps_ref, all_ref.at[:, mine], tsend.at[d], trecv.at[d], around[d]) for d in range(3)]
+        all_ref[:, mine] = taps_ref[...]
         out_ref[:, pl.ds(pl.multiple_of((row * 4 + col) * width, width), width)] = own_ref[...]
         gather_plane(own_ref, out_ref, send, recv)
+        for copy in made:
+            copy.wait_recv()
+        for copy in made:
+            copy.wait_send()
 
     return pl.pallas_call(
         kernel,
-        out_shape=jax.ShapeDtypeStruct((rows, width * 16), own.dtype),
-        in_specs=[VM],
-        out_specs=VM,
-        scratch_shapes=[DMA((15,)), DMA((15,))],
+        out_shape=(
+            jax.ShapeDtypeStruct((rows, width * 16), own.dtype),
+            jax.ShapeDtypeStruct((deep, share * 4), taps.dtype),
+        ),
+        in_specs=[VM, VM],
+        out_specs=(VM, VM),
+        scratch_shapes=[DMA((15,)), DMA((15,)), DMA((3,)), DMA((3,))],
         compiler_params=params(1),
         name="gather_tokens",
-    )(own)
+    )(own, taps)
 
 
 def gather_head(branch):
@@ -169,8 +177,8 @@
         if gather:
             out_ref, gsend, grecv = refs[3], refs[-2], refs[-1]
             refs = refs[:3] + refs[4:-2]
-        (got, got_a, got_b, got_small, got_edges, going, state_ref, total, chosen, upright, hidden, stat, got_stat,
-         gated, term, near, held, far, last, pair, send, recv, esend, erecv, local) = refs[3:]
+        (got, got_a, twin, paired, got_b, got_small, got_edges, going, state_ref, total, chosen, upright, hidden, stat,
+         got_stat, gated, term, near, held, far, last, pair, send, recv, esend, erecv, local) = refs[3:]
         place = lax.axis_index("seq")
         row, col, core, cross, mate = plane()
         peers = [lax.rem(place + d, SEQ) for d in range(SEQ)]
@@ -186,10 +194,17 @@
             arrive.append(copy_to(small_ref, got_small.at[place], send.at[0, d], recv.at[0, d], to))
             arrive.append(copy_to(sums_ref.at[peers[d], :, inc], got.at[place], send.at[1, d], recv.at[1, d], to))
         sent += arrive
+        odd = lax.rem(place, 2)
+        level = lax.div(place, 2)
+        beside = {"seq": place + 1 - 2 * odd}
+        twins = [
+            copy_to(sums_ref.at[2 * i + 1 - odd, :, end_a], twin.at[i], send.at[2, 8 + i], recv.at[2, 8 + i], beside)
+            for i in range(8)
+        ]
+        sent += twins
         own = [
             pltpu.make_async_copy(small_ref, got_small.at[place], local.at[0]),
             pltpu.make_async_copy(sums_ref.at[place, :, inc], got.at[place], local.at[1]),
-            pltpu.make_async_copy(sums_ref.at[place, :, end_a], got_a.at[place], local.at[2]),
             pltpu.make_async_copy(edges_ref, got_edges.at[place], local.at[3]),
         ]
         for made in own:
@@ -243,13 +258,21 @@
         ]
         sent += arrive
         state_ref[place] = going[place]
+        for i in range(8):
+            twins[i].wait_recv()
+            mine = sums_ref[2 * i + odd, :, cols : 2 * cols]
+            paired[i] = (mine.astype(jnp.float32) + twin[i].astype(jnp.float32)).astype(jnp.bfloat16)
+        got_a[level] = paired[level]
         for made in arrive:
             made.wait_recv()
         late = []
+        for d in range(1, 8):
+            to = lax.rem(level + d, 8)
+            late.append(
+                copy_to(paired.at[to], got_a.at[level], send.at[2, d], recv.at[2, d], {"seq": 2 * to + odd})
+            )
         for d in range(1, SEQ):
-            to = {"seq": peers[d]}
-            late.append(copy_to(edges_ref, got_edges.at[place], send.at[5, d], recv.at[5, d], to))
-            late.append(copy_to(sums_ref.at[peers[d], :, end_a], got_a.at[place], send.at[2, d], recv.at[2, d], to))
+            late.append(copy_to(edges_ref, got_edges.at[place], send.at[5, d], recv.at[5, d], {"seq": peers[d]}))
         sent += late
         b_copies = [
             pltpu.make_async_remote_copy(
@@ -308,6 +331,46 @@
                         near.at[2 * d + h], send.at[6, 2 * d + h], recv.at[6, 2 * d + h], {"wc": mate},
                     )
                 )
+        for made in late:
+            made.wait_recv()
+
+        @pl.when(place != SPLIT)
+        def _():
+            b_copies[0].wait_recv()
+
+        whole_a, whole_b, third = total[0], total[1] + got_b[...].astype(jnp.float32), total[2]
+        edge = jnp.zeros((16, cols), jnp.float32)
+        for k in range(SEQ):
+            edge = edge + got_edges[k].astype(jnp.float32)
+        for k in range(8):
+            if 2 * k <= SPLIT:
+                whole_a = whole_a + got_a[k].astype(jnp.float32)
+            else:
+                whole_b = whole_b + got_a[k].astype(jnp.float32)
+        total[0] = whole_a
+        total[1] = whole_b
+        side = []
+        for d in range(1, SEQ):
+            for j in range(2):
+                which = got_small[peers[d], 3 + j : 4 + j]
+                which = jnp.concatenate([which] * (cols // 128), axis=1)
+                chosen[peers[d], j] = jnp.where(
+                    which == 0.0, total[0], jnp.where(which == 1.0, total[1], total[2])
+                ).astype(jnp.bfloat16)
+            side.append(
+                copy_to(chosen.at[peers[d]], req_ref.at[:, place], send.at[7, d], recv.at[7, d], {"seq": peers[d]})
+            )
+        for j in range(2):
+            which = small_ref[3 + j : 4 + j]
+            which = jnp.concatenate([which] * (cols // 128), axis=1)
+            req_ref[j, place] = jnp.where(
+                which == 0.0, total[0], jnp.where(which == 1.0, total[1], total[2])
+            ).astype(jnp.bfloat16)
+            edge_ref[j, 0:3] = jnp.where(
+                which == 0.0, edge[0:3], jnp.where(which == 1.0, edge[3:6], edge[6:9])
+            )
+        sent += side
+
         second = []
         for i, d in enumerate(order):
             for h in range(2):
@@ -324,45 +387,6 @@
                 )
         sent += first + second
 
-        for made in late:
-            made.wait_recv()
-
-        @pl.when(place != SPLIT)
-        def _():
-            b_copies[0].wait_recv()
-
-        first, second_end, third = total[0], total[1] + got_b[...].astype(jnp.float32), total[2]
-        edge = jnp.zeros((16, cols), jnp.float32)
-        for k in range(SEQ):
-            edge = edge + got_edges[k].astype(jnp.float32)
-            if k <= SPLIT:
-                first = first + got_a[k].astype(jnp.float32)
-            else:
-                second_end = second_end + got_a[k].astype(jnp.float32)
-        total[0] = first
-        total[1] = second_end
-        side = []
-        for d in range(1, SEQ):
-            for j in range(2):
-                which = got_small[peers[d], 3 + j : 4 + j]
-                which = jnp.concatenate([which] * (cols // 128), axis=1)
-                chosen[peers[d], j] = jnp.where(
-                    which == 0.0, total[0], jnp.where(which == 1.0, total[1], total[2])
-                ).astype(jnp.bfloat16)
-            side.append(
-                copy_to(chosen.at[peers[d]], req_ref.at[:, place], send.at[7, d], recv.at[7, d], {"seq": peers[d]})
-            )
-        for j in range(2):
-            which = small_ref[3 + j : 4 + j]
-            which = jnp.concatenate([which] * (cols // 128), axis=1)
-            req_ref[j, place] = jnp.where(
-                which == 0.0, total[0], jnp.where(which == 1.0, total[1], total[2])
-            ).astype(jnp.bfloat16)
-            edge_ref[j, 0:3] = jnp.where(
-                which == 0.0, edge[0:3], jnp.where(which == 1.0, edge[3:6], edge[6:9])
-            )
-        sent += side
-
         for made in second:
             made.wait_recv()
         other = lax.rem(lax.div(col, 2) + 1, 2)
@@ -401,7 +425,9 @@
     ]
     scratch = [
         pltpu.VMEM((spans, part, cols), b16),
-        pltpu.VMEM((spans, part, cols), b16),
+        pltpu.VMEM((8, part, cols), b16),
+        pltpu.VMEM((8, part, cols), b16),
+        pltpu.VMEM((8, part, cols), b16),
         pltpu.VMEM((part, cols), b16),
         pltpu.VMEM((spans, 8, 128), f32),
         pltpu.VMEM((spans, 16, cols), b16),
@@ -494,10 +520,11 @@
     local_ends = [jnp.clip(end - row_offset, 0, tok_rows - 1) for end in ends]
     head_mask = (jnp.arange(HEADS, dtype=jnp.int32) == head_idx).astype(jnp.float32)
     row_order = jnp.arange(tok_rows)
-    conv_all = jnp.concatenate([conv_weight, conv_bias[:, None]], axis=1)
-    conv_all = lax.all_gather(conv_all, "wc", axis=2, tiled=True)
+    taps = jnp.concatenate(
+        [conv_weight.reshape(LAYERS * CONV, -1), conv_bias, jnp.zeros((6, conv_bias.shape[1]), jnp.float32)], axis=0
+    )
     current = tokens
-    gathered = gather16(tokens)
+    gathered, taps_all = gather16(tokens, taps)
     states = []
     edges_out = []
     for layer in range(LAYERS):
@@ -512,7 +539,9 @@
         head_branch, rim = gather_head(branch)
         width = branch.shape[1]
         extended = jnp.concatenate([rim[rim.shape[0] - (CONV - 1) :], head_branch], axis=0)
-        head_act = conv_rows(extended, ext_segment, segment, conv_all[layer, :CONV], conv_all[layer, CONV])
+        head_act = conv_rows(
+            extended, ext_segment, segment, taps_all[layer * CONV : (layer + 1) * CONV], taps_all[LAYERS * CONV + layer]
+        )
         head_width = head_act.shape[1]
         queries = block_mix(head_act, w_query[layer, 0]).astype(jnp.bfloat16)
         key_rows = (block_mix(head_act, w_key[layer, 0]) * head_width ** (-0.5)).astype(jnp.bfloat16)

time: 306 us -> 302 us (0.987)
  blocking collectives: 6.75 us -> 0 us
    all_gather x1 -> x0, blocking collectives: 6.75 us -> none  [body(): conv_all = lax.all_gather(conv_all, 'wc', axis=2, tiled=True)]
    unnamed x154 -> x256, local copies, waits for them, and re-layouts: 7.64 us -> 5.39 us
where the time goes in v3:
time: 302 us; the launch traced here: 298 us
  Pallas kernels  214 us (71%)
  other arithmetic  34.4 us (11%)
  local copies, waits for them, and re-layouts  24.9 us (8%)
  matrix products  14.2 us (5%)
  between operations  10.2 us (3%)
    pallas_call x2, Pallas kernels, tail(): pl.pallas_call(kernel, out_shape=tuple(shapes), in_specs=[VM] * 12, out_s...  171 us
    pallas_call x2, Pallas kernels, gather_head(): pl.pallas_call(kernel, out_shape=(jax.ShapeDtypeStruct((rows, width * 4),...  23.6 us
    pallas_call x1, Pallas kernels, gather16(): pl.pallas_call(kernel, out_shape=(jax.ShapeDtypeStruct((rows, width * 16)...  19.2 us

profile of v3, /device:TPU:8, one launch (start us, length us, event | category | flops | bytes accessed | tf_op | source)
XLA Modules:
  0.0 297.7 jit_solution(2521819038475471843)
XLA Ops:
  1.5 1.3 slice_bitcast_fusion.6
  2.8 1.3 fusion.96
  11.2 1.3 fusion.78
  16.1 1.4 fusion.91
  17.5 1.4 fusion.88
  23.0 1.7 slice_bitcast_fusion
  24.7 19.2 %gather_tokens.1 = (bf16[512,2048]{1,0:T(8,128)(2,1)S(1)}, f32[16,1024]{1,0:T(8,128)S(1)}) custom-call(bf16[512,128]{1,0:T(8,128)(2,1)S(1)} %copy-done.3, f32[16,256]{1,0:T(8,128)S(1)} %maximum_maximum_fusion.taps_ref), custom_call_target="tpu_custom_call" | custom-call | tf_op jit(solution)/shard_map/gather_tokens/pallas_call | solution.py:105
  46.0 1.3 copy-done.11
  52.2 2.0 broadcast_subtract_fusion.5
  56.7 2.7 convolution_convert_fusion.3.own_ref
  59.9 1.5 fusion.29.og_ref
  61.4 11.6 %gather_head.2 = (bf16[512,1024]{1,0:T(8,128)(2,1)S(1)}, bf16[16,1024]{1,0:T(8,128)(2,1)S(1)}) custom-call(bf16[512,256]{1,0:T(8,128)(2,1)S(1)} %convolution_convert_fusion.3.own_ref), custom_call_target="tpu_custom_call" | custom-call | tf_op jit(solution)/shard_map/gather_head/pallas_call | solution.py:150
  77.7 2.1 fusion.84
  82.5 2.2 convolution_convert_fusion.1
  84.7 95.9 %tail_gather.1 = (bf16[512,128]{1,0:T(8,128)(2,1)S(1)}, bf16[2,16,64,256]{3,2,1,0:T(8,128)(2,1)S(1)}, f32[2,8,256]{2,1,0:T(8,128)S(1)}, bf16[512,2048]{1,0:T(8,128)(2,1)}) custom-call(bf16[16,64,768]{2,1,0:T(8,128)(2,1)} %bitcast.207, f32[8,128]{1,0:T(8,128)S(1)} %copy-done.7, bf16[16,256]{1,0:T(8,128)(2,1)S(1)} %copy-done.6, f32[8,512]{1,0:T(8,128)S(1)} %stack.66.lines_ref, ...), custom_call_target="tpu_custom_call" | custom-call | tf_op jit(solution)/shard_map/tail_gather/pallas_call | solution.py:454
  180.7 2.7 convert_reduce_fusion
  189.2 1.9 broadcast_subtract_fusion.2
  192.4 2.1 convolution_convert_fusion.2.own_ref
  194.6 2.3 fusion.26.og_ref
  196.9 12.0 %gather_head.3 = (bf16[512,1024]{1,0:T(8,128)(2,1)S(1)}, bf16[16,1024]{1,0:T(8,128)(2,1)S(1)}) custom-call(bf16[512,256]{1,0:T(8,128)(2,1)S(1)} %convolution_convert_fusion.2.own_ref), custom_call_target="tpu_custom_call" | custom-call | tf_op jit(solution)/shard_map/gather_head/pallas_call | solution.py:150
  212.5 2.3 fusion.83
  217.4 2.2 convolution_convert_fusion
  219.6 75.3 %tail_last.1 = (bf16[512,128]{1,0:T(8,128)(2,1)S(1)}, bf16[2,16,64,256]{3,2,1,0:T(8,128)(2,1)S(1)}, f32[2,8,256]{2,1,0:T(8,128)S(1)}) custom-call(bf16[16,64,768]{2,1,0:T(8,128)(2,1)} %bitcast.208, f32[8,128]{1,0:T(8,128)S(1)} %broadcast_in_dim.88.small_ref, bf16[16,256]{1,0:T(8,128)(2,1)S(1)} %maximum_maximum_fusion.2.edges_ref, ...), custom_call_target="tpu_custom_call" | custom-call | tf_op jit(solution)/shard_map/tail_last/pallas_call | solution.py:454
  294.9 1.5 pad_maximum_fusion.2
  (354 shorter events, 38.3 us)
Async XLA Ops:
  0.7 47.3 %copy-start.116 = (f32[4]{0:T(128)}, f32[4]{0:T(128)S(1)}, u32[]{:S(2)}) copy-start(f32[4]{0:T(128)S(1)} %compare_convert_fusion.4) | copy-start | bytes 52
  1.3 50.0 %copy-start.119 = (f32[2]{0:T(128)}, f32[2]{0:T(128)S(1)}, u32[]{:S(2)}) copy-start(f32[2]{0:T(128)S(1)} %convert_element_type.255) | copy-start | bytes 28
  1.5 71.7 %copy-start.123 = (bf16[16]{0:T(256)(128)(2,1)}, bf16[16]{0:T(256)(128)(2,1)S(1)}, u32[]{:S(2)}) copy-start(bf16[16]{0:T(256)(128)(2,1)S(1)} %pad.32.clone) | copy-start | bytes 100
  7.4 65.6 %copy-start.114 = (pred[3]{0:T(512)(128)(4,1)}, pred[3]{0:T(512)(128)(4,1)S(1)}, u32[]{:S(2)}) copy-start(pred[3]{0:T(512)(128)(4,1)S(1)} %compare_and_fusion.4) | copy-start | bytes 13
  8.7 64.3 %copy-start.38 = (pred[3]{0:T(512)(128)(4,1)}, pred[3]{0:T(512)(128)(4,1)S(1)}, u32[]{:S(2)}) copy-start(pred[3]{0:T(512)(128)(4,1)S(1)} %get-tuple-element.192) | copy-start | bytes 13
  8.7 64.3 %copy-start.40 = (pred[3]{0:T(512)(128)(4,1)}, pred[3]{0:T(512)(128)(4,1)S(1)}, u32[]{:S(2)}) copy-start(pred[3]{0:T(512)(128)(4,1)S(1)} %get-tuple-element.193) | copy-start | bytes 13
  9.4 47.3 %copy-start.20 = (f32[1,512]{1,0:T(1,128)}, f32[1,512]{1,0:T(1,128)S(1)}, u32[]{:S(2)}) copy-start(f32[1,512]{1,0:T(1,128)S(1)} %fusion.81) | copy-start | bytes 6148
  51.4 2.8 copy-start.121
  56.7 2.8 copy-start.15
  56.7 3.2 %copy-start.125 = (bf16[2,2048,256]{2,1,0:T(8,128)(2,1)S(1)}, bf16[2,2048,256]{2,1,0:T(8,128)(2,1)}, u32[]{:S(2)}) copy-start(bf16[2,2048,256]{2,1,0:T(8,128)(2,1)} %param.19) | copy-start | bytes 6291460
  180.6 3.5 %copy-start = (bf16[2,16,64,256]{3,2,1,0:T(8,128)(2,1)}, bf16[2,16,64,256]{3,2,1,0:T(8,128)(2,1)S(1)}, u32[]{:S(2)}) copy-start(bf16[2,16,64,256]{3,2,1,0:T(8,128)(2,1)S(1)} %get-tuple-element.25) | copy-start | bytes 3145732
  180.6 3.5 %copy-start.4 = (bf16[512,128]{1,0:T(8,128)(2,1)}, bf16[512,128]{1,0:T(8,128)(2,1)S(1)}, u32[]{:S(2)}) copy-start(bf16[512,128]{1,0:T(8,128)(2,1)S(1)} %get-tuple-element.23.cur_ref) | copy-start | bytes 393220
  180.6 2.8 copy-start.13
  180.6 2.8 copy-start.19
  184.3 8.1 %copy-start.10 = (bf16[512,2048]{1,0:T(8,128)(2,1)}, bf16[512,2048]{1,0:T(8,128)(2,1)S(1)}, u32[]{:S(2)}) copy-start(bf16[512,2048]{1,0:T(8,128)(2,1)S(1)} %fusion.6) | copy-start | bytes 6291460
  184.3 4.1 %copy-start.120 = (f32[2]{0:T(128)S(1)}, f32[2]{0:T(128)}, u32[]{:S(2)}) copy-start(f32[2]{0:T(128)} %copy-done.119) | copy-start | bytes 28
  184.3 4.1 %copy-start.122 = (f32[3]{0:T(128)S(1)}, f32[3]{0:T(128)}, u32[]{:S(2)}) copy-start(f32[3]{0:T(128)} %copy-done.121) | copy-start | bytes 40
  184.3 4.9 %copy-start.16 = (f32[4,512]{1,0:T(4,128)S(1)}, f32[4,512]{1,0:T(4,128)}, u32[]{:S(2)}) copy-start(f32[4,512]{1,0:T(4,128)} %copy-done.15) | copy-start | bytes 24580
  184.3 4.9 %copy-start.21 = (f32[1,512]{1,0:T(1,128)S(1)}, f32[1,512]{1,0:T(1,128)}, u32[]{:S(2)}) copy-start(f32[1,512]{1,0:T(1,128)} %copy-done.20) | copy-start | bytes 6148
  194.5 14.4 %copy-start.39 = (pred[3]{0:T(512)(128)(4,1)S(1)}, pred[3]{0:T(512)(128)(4,1)}, u32[]{:S(2)}) copy-start(pred[3]{0:T(512)(128)(4,1)} %copy-done.38) | copy-start | bytes 13
  194.5 14.4 %copy-start.41 = (pred[3]{0:T(512)(128)(4,1)S(1)}, pred[3]{0:T(512)(128)(4,1)}, u32[]{:S(2)}) copy-start(pred[3]{0:T(512)(128)(4,1)} %copy-done.40) | copy-start | bytes 13
  194.5 14.4 %copy-start.115 = (pred[3]{0:T(512)(128)(4,1)S(1)}, pred[3]{0:T(512)(128)(4,1)}, u32[]{:S(2)}) copy-start(pred[3]{0:T(512)(128)(4,1)} %copy-done.114) | copy-start | bytes 13
  194.6 14.6 %copy-start.124 = (bf16[16]{0:T(256)(128)(2,1)S(1)}, bf16[16]{0:T(256)(128)(2,1)}, u32[]{:S(2)}) copy-start(bf16[16]{0:T(256)(128)(2,1)} %copy-done.123) | copy-start | bytes 100
  219.6 75.3 %copy-start.1 = (bf16[2,16,64,256]{3,2,1,0:T(8,128)(2,1)S(1)}, bf16[2,16,64,256]{3,2,1,0:T(8,128)(2,1)}, u32[]{:S(2)}) copy-start(bf16[2,16,64,256]{3,2,1,0:T(8,128)(2,1)} %copy-done) | copy-start | bytes 3145732
  (103 other events, 135.1 us)

commit v4 on v3

--- a/solution.py
+++ b/solution.py
@@ -316,6 +316,47 @@
                 (normal * gains_ref[0:1] + gains_ref[1:2] * act_ref[at].astype(jnp.float32)) * (gate * jax.nn.sigmoid(gate))
             ).astype(jnp.bfloat16)
 
+        def deliver():
+            for made in late:
+                made.wait_recv()
+
+            @pl.when(place != SPLIT)
+            def _():
+                b_copies[0].wait_recv()
+
+            whole_a, whole_b, third = total[0], total[1] + got_b[...].astype(jnp.float32), total[2]
+            edge = jnp.zeros((16, cols), jnp.float32)
+            for k in range(SEQ):
+                edge = edge + got_edges[k].astype(jnp.float32)
+            for k in range(8):
+                if 2 * k <= SPLIT:
+                    whole_a = whole_a + got_a[k].astype(jnp.float32)
+                else:
+                    whole_b = whole_b + got_a[k].astype(jnp.float32)
+            total[0] = whole_a
+            total[1] = whole_b
+            side = []
+            for d in range(1, SEQ):
+                for j in range(2):
+                    which = got_small[peers[d], 3 + j : 4 + j]
+                    which = jnp.concatenate([which] * (cols // 128), axis=1)
+                    chosen[peers[d], j] = jnp.where(
+                        which == 0.0, total[0], jnp.where(which == 1.0, total[1], total[2])
+                    ).astype(jnp.bfloat16)
+                side.append(
+                    copy_to(chosen.at[peers[d]], req_ref.at[:, place], send.at[7, d], recv.at[7, d], {"seq": peers[d]})
+                )
+            for j in range(2):
+                which = small_ref[3 + j : 4 + j]
+                which = jnp.concatenate([which] * (cols // 128), axis=1)
+                req_ref[j, place] = jnp.where(
+                    which == 0.0, total[0], jnp.where(which == 1.0, total[1], total[2])
+                ).astype(jnp.bfloat16)
+                edge_ref[j, 0:3] = jnp.where(
+                    which == 0.0, edge[0:3], jnp.where(which == 1.0, edge[3:6], edge[6:9])
+                )
+            return side
+
         order = [2, 1, 3, 0]
         rows_to = [lax.rem(row + d, 4) for d in range(4)]
         first = []
@@ -331,46 +372,7 @@
                         near.at[2 * d + h], send.at[6, 2 * d + h], recv.at[6, 2 * d + h], {"wc": mate},
                     )
                 )
-        for made in late:
-            made.wait_recv()
-
-        @pl.when(place != SPLIT)
-        def _():
-            b_copies[0].wait_recv()
-
-        whole_a, whole_b, third = total[0], total[1] + got_b[...].astype(jnp.float32), total[2]
-        edge = jnp.zeros((16, cols), jnp.float32)
-        for k in range(SEQ):
-            edge = edge + got_edges[k].astype(jnp.float32)
-        for k in range(8):
-            if 2 * k <= SPLIT:
-                whole_a = whole_a + got_a[k].astype(jnp.float32)
-            else:
-                whole_b = whole_b + got_a[k].astype(jnp.float32)
-        total[0] = whole_a
-        total[1] = whole_b
-        side = []
-        for d in range(1, SEQ):
-            for j in range(2):
-                which = got_small[peers[d], 3 + j : 4 + j]
-                which = jnp.concatenate([which] * (cols // 128), axis=1)
-                chosen[peers[d], j] = jnp.where(
-                    which == 0.0, total[0], jnp.where(which == 1.0, total[1], total[2])
-                ).astype(jnp.bfloat16)
-            side.append(
-                copy_to(chosen.at[peers[d]], req_ref.at[:, place], send.at[7, d], recv.at[7, d], {"seq": peers[d]})
-            )
-        for j in range(2):
-            which = small_ref[3 + j : 4 + j]
-            which = jnp.concatenate([which] * (cols // 128), axis=1)
-            req_ref[j, place] = jnp.where(
-                which == 0.0, total[0], jnp.where(which == 1.0, total[1], total[2])
-            ).astype(jnp.bfloat16)
-            edge_ref[j, 0:3] = jnp.where(
-                which == 0.0, edge[0:3], jnp.where(which == 1.0, edge[3:6], edge[6:9])
-            )
-        sent += side
-
+        side = [] if gather else deliver()
         second = []
         for i, d in enumerate(order):
             for h in range(2):
@@ -387,6 +389,9 @@
                 )
         sent += first + second
 
+        if gather:
+            side = deliver()
+        sent += side
         for made in second:
             made.wait_recv()
         other = lax.rem(lax.div(col, 2) + 1, 2)

time: 302 us -> 293 us (0.970)
  Pallas kernels: 214 us -> 206 us
    pallas_call x2, Pallas kernels: 171 us -> 163 us  [tail(): pl.pallas_call(kernel, out_shape=tuple(shapes), in_specs=[VM] * 12, out_s...]
where the time goes in v4:
time: 293 us; the launch traced here: 290 us
  Pallas kernels  206 us (70%)
  other arithmetic  34.4 us (12%)
  local copies, waits for them, and re-layouts  24.9 us (8%)
  matrix products  14.2 us (5%)
  between operations  10.2 us (3%)
    pallas_call x2, Pallas kernels, tail(): pl.pallas_call(kernel, out_shape=tuple(shapes), in_specs=[VM] * 12, out_s...  163 us
    pallas_call x2, Pallas kernels, gather_head(): pl.pallas_call(kernel, out_shape=(jax.ShapeDtypeStruct((rows, width * 4),...  24.1 us
    pallas_call x1, Pallas kernels, gather16(): pl.pallas_call(kernel, out_shape=(jax.ShapeDtypeStruct((rows, width * 16)...  19.2 us

profile of v4, /device:TPU:8, one launch (start us, length us, event | category | flops | bytes accessed | tf_op | source)
XLA Modules:
  0.0 290.2 jit_solution(3770420324141607531)
XLA Ops:
  1.5 1.3 slice_bitcast_fusion.6
  2.8 1.3 fusion.96
  11.2 1.3 fusion.78
  16.1 1.4 fusion.91
  17.5 1.4 fusion.88
  23.0 1.7 slice_bitcast_fusion
  24.7 19.2 %gather_tokens.1 = (bf16[512,2048]{1,0:T(8,128)(2,1)S(1)}, f32[16,1024]{1,0:T(8,128)S(1)}) custom-call(bf16[512,128]{1,0:T(8,128)(2,1)S(1)} %copy-done.3, f32[16,256]{1,0:T(8,128)S(1)} %maximum_maximum_fusion.taps_ref), custom_call_target="tpu_custom_call" | custom-call | tf_op jit(solution)/shard_map/gather_tokens/pallas_call | solution.py:105
  46.0 1.3 copy-done.11
  52.2 2.0 broadcast_subtract_fusion.5
  56.7 2.7 convolution_convert_fusion.3.own_ref
  59.9 1.5 fusion.29.og_ref
  61.4 11.6 %gather_head.2 = (bf16[512,1024]{1,0:T(8,128)(2,1)S(1)}, bf16[16,1024]{1,0:T(8,128)(2,1)S(1)}) custom-call(bf16[512,256]{1,0:T(8,128)(2,1)S(1)} %convolution_convert_fusion.3.own_ref), custom_call_target="tpu_custom_call" | custom-call | tf_op jit(solution)/shard_map/gather_head/pallas_call | solution.py:150
  77.7 2.1 fusion.84
  82.5 2.2 convolution_convert_fusion.1
  84.7 85.3 %tail_gather.1 = (bf16[512,128]{1,0:T(8,128)(2,1)S(1)}, bf16[2,16,64,256]{3,2,1,0:T(8,128)(2,1)S(1)}, f32[2,8,256]{2,1,0:T(8,128)S(1)}, bf16[512,2048]{1,0:T(8,128)(2,1)}) custom-call(bf16[16,64,768]{2,1,0:T(8,128)(2,1)} %bitcast.207, f32[8,128]{1,0:T(8,128)S(1)} %copy-done.7, bf16[16,256]{1,0:T(8,128)(2,1)S(1)} %copy-done.6, f32[8,512]{1,0:T(8,128)S(1)} %stack.66.lines_ref, ...), custom_call_target="tpu_custom_call" | custom-call | tf_op jit(solution)/shard_map/tail_gather/pallas_call | solution.py:459
  170.1 2.7 convert_reduce_fusion
  178.6 1.9 broadcast_subtract_fusion.2
  181.8 2.1 convolution_convert_fusion.2.own_ref
  184.0 2.3 fusion.26.og_ref
  186.3 12.5 %gather_head.3 = (bf16[512,1024]{1,0:T(8,128)(2,1)S(1)}, bf16[16,1024]{1,0:T(8,128)(2,1)S(1)}) custom-call(bf16[512,256]{1,0:T(8,128)(2,1)S(1)} %convolution_convert_fusion.2.own_ref), custom_call_target="tpu_custom_call" | custom-call | tf_op jit(solution)/shard_map/gather_head/pallas_call | solution.py:150
  202.3 2.3 fusion.83
  207.3 2.2 convolution_convert_fusion
  209.5 77.9 %tail_last.1 = (bf16[512,128]{1,0:T(8,128)(2,1)S(1)}, bf16[2,16,64,256]{3,2,1,0:T(8,128)(2,1)S(1)}, f32[2,8,256]{2,1,0:T(8,128)S(1)}) custom-call(bf16[16,64,768]{2,1,0:T(8,128)(2,1)} %bitcast.208, f32[8,128]{1,0:T(8,128)S(1)} %broadcast_in_dim.88.small_ref, bf16[16,256]{1,0:T(8,128)(2,1)S(1)} %maximum_maximum_fusion.2.edges_ref, ...), custom_call_target="tpu_custom_call" | custom-call | tf_op jit(solution)/shard_map/tail_last/pallas_call | solution.py:459
  287.4 1.5 pad_maximum_fusion.2
  (354 shorter events, 38.3 us)
Async XLA Ops:
  0.7 47.3 %copy-start.116 = (f32[4]{0:T(128)}, f32[4]{0:T(128)S(1)}, u32[]{:S(2)}) copy-start(f32[4]{0:T(128)S(1)} %compare_convert_fusion.4) | copy-start | bytes 52
  1.3 50.0 %copy-start.119 = (f32[2]{0:T(128)}, f32[2]{0:T(128)S(1)}, u32[]{:S(2)}) copy-start(f32[2]{0:T(128)S(1)} %convert_element_type.255) | copy-start | bytes 28
  1.5 71.7 %copy-start.123 = (bf16[16]{0:T(256)(128)(2,1)}, bf16[16]{0:T(256)(128)(2,1)S(1)}, u32[]{:S(2)}) copy-start(bf16[16]{0:T(256)(128)(2,1)S(1)} %pad.32.clone) | copy-start | bytes 100
  7.4 65.6 %copy-start.114 = (pred[3]{0:T(512)(128)(4,1)}, pred[3]{0:T(512)(128)(4,1)S(1)}, u32[]{:S(2)}) copy-start(pred[3]{0:T(512)(128)(4,1)S(1)} %compare_and_fusion.4) | copy-start | bytes 13
  8.7 64.3 %copy-start.38 = (pred[3]{0:T(512)(128)(4,1)}, pred[3]{0:T(512)(128)(4,1)S(1)}, u32[]{:S(2)}) copy-start(pred[3]{0:T(512)(128)(4,1)S(1)} %get-tuple-element.192) | copy-start | bytes 13
  8.7 64.3 %copy-start.40 = (pred[3]{0:T(512)(128)(4,1)}, pred[3]{0:T(512)(128)(4,1)S(1)}, u32[]{:S(2)}) copy-start(pred[3]{0:T(512)(128)(4,1)S(1)} %get-tuple-element.193) | copy-start | bytes 13
  9.4 47.3 %copy-start.20 = (f32[1,512]{1,0:T(1,128)}, f32[1,512]{1,0:T(1,128)S(1)}, u32[]{:S(2)}) copy-start(f32[1,512]{1,0:T(1,128)S(1)} %fusion.81) | copy-start | bytes 6148
  51.4 2.8 copy-start.121
  56.7 2.8 copy-start.15
  56.7 3.2 %copy-start.125 = (bf16[2,2048,256]{2,1,0:T(8,128)(2,1)S(1)}, bf16[2,2048,256]{2,1,0:T(8,128)(2,1)}, u32[]{:S(2)}) copy-start(bf16[2,2048,256]{2,1,0:T(8,128)(2,1)} %param.19) | copy-start | bytes 6291460
  170.0 3.5 %copy-start = (bf16[2,16,64,256]{3,2,1,0:T(8,128)(2,1)}, bf16[2,16,64,256]{3,2,1,0:T(8,128)(2,1)S(1)}, u32[]{:S(2)}) copy-start(bf16[2,16,64,256]{3,2,1,0:T(8,128)(2,1)S(1)} %get-tuple-element.25) | copy-start | bytes 3145732
  170.0 3.5 %copy-start.4 = (bf16[512,128]{1,0:T(8,128)(2,1)}, bf16[512,128]{1,0:T(8,128)(2,1)S(1)}, u32[]{:S(2)}) copy-start(bf16[512,128]{1,0:T(8,128)(2,1)S(1)} %get-tuple-element.23.cur_ref) | copy-start | bytes 393220
  170.0 2.8 copy-start.13
  170.0 2.8 copy-start.19
  173.7 8.1 %copy-start.10 = (bf16[512,2048]{1,0:T(8,128)(2,1)}, bf16[512,2048]{1,0:T(8,128)(2,1)S(1)}, u32[]{:S(2)}) copy-start(bf16[512,2048]{1,0:T(8,128)(2,1)S(1)} %fusion.6) | copy-start | bytes 6291460
  173.7 4.1 %copy-start.120 = (f32[2]{0:T(128)S(1)}, f32[2]{0:T(128)}, u32[]{:S(2)}) copy-start(f32[2]{0:T(128)} %copy-done.119) | copy-start | bytes 28
  173.7 4.1 %copy-start.122 = (f32[3]{0:T(128)S(1)}, f32[3]{0:T(128)}, u32[]{:S(2)}) copy-start(f32[3]{0:T(128)} %copy-done.121) | copy-start | bytes 40
  173.7 4.9 %copy-start.16 = (f32[4,512]{1,0:T(4,128)S(1)}, f32[4,512]{1,0:T(4,128)}, u32[]{:S(2)}) copy-start(f32[4,512]{1,0:T(4,128)} %copy-done.15) | copy-start | bytes 24580
  173.7 4.9 %copy-start.21 = (f32[1,512]{1,0:T(1,128)S(1)}, f32[1,512]{1,0:T(1,128)}, u32[]{:S(2)}) copy-start(f32[1,512]{1,0:T(1,128)} %copy-done.20) | copy-start | bytes 6148
  183.9 14.9 %copy-start.39 = (pred[3]{0:T(512)(128)(4,1)S(1)}, pred[3]{0:T(512)(128)(4,1)}, u32[]{:S(2)}) copy-start(pred[3]{0:T(512)(128)(4,1)} %copy-done.38) | copy-start | bytes 13
  183.9 14.9 %copy-start.41 = (pred[3]{0:T(512)(128)(4,1)S(1)}, pred[3]{0:T(512)(128)(4,1)}, u32[]{:S(2)}) copy-start(pred[3]{0:T(512)(128)(4,1)} %copy-done.40) | copy-start | bytes 13
  183.9 14.9 %copy-start.115 = (pred[3]{0:T(512)(128)(4,1)S(1)}, pred[3]{0:T(512)(128)(4,1)}, u32[]{:S(2)}) copy-start(pred[3]{0:T(512)(128)(4,1)} %copy-done.114) | copy-start | bytes 13
  183.9 15.1 %copy-start.124 = (bf16[16]{0:T(256)(128)(2,1)S(1)}, bf16[16]{0:T(256)(128)(2,1)}, u32[]{:S(2)}) copy-start(bf16[16]{0:T(256)(128)(2,1)} %copy-done.123) | copy-start | bytes 100
  209.4 78.0 %copy-start.1 = (bf16[2,16,64,256]{3,2,1,0:T(8,128)(2,1)S(1)}, bf16[2,16,64,256]{3,2,1,0:T(8,128)(2,1)}, u32[]{:S(2)}) copy-start(bf16[2,16,64,256]{3,2,1,0:T(8,128)(2,1)} %copy-done) | copy-start | bytes 3145732
  (103 other events, 135.1 us)
